TPU v7x, 512 devices: a whole 4x8x8 slice. The times are simulated.
512 devices in a mesh: blk: 128 (over z, y, core), head: 4 (over x).
Axes of the slice: x: 4, y: 8, z: 8, core: 2. Of those that a mesh axis runs over, the one named last changes fastest.
Arguments:
- layer_entry_vectors: bfloat16 [1024, 16, 2048], P('blk', None, 'head'), may hold values from -6 to 6
- guessed_lookup_vectors: bfloat16 [1024, 16, 2048], P('blk', None, 'head'), may hold values from -3 to 3
- guessed_content_vectors: bfloat16 [1024, 16, 2048], P('blk', None, 'head'), may hold values from -6 to 6
- gating_query: bfloat16 [1024, 16, 2048], P('blk', 'head'), may hold values from -6 to 6
- lane_memory_store: float32 [4, 16384, 2048], P('head', 'blk'), may hold values from -3 to 3
- prior_step_store: float32 [4, 16384, 32], P('head', 'blk'), may hold values from -6 to 6
- fading_blend_ratio: float32 [2048], P('head'), may hold values from 0 to 1
- learning_speed_blend: float32 [2048], P('head'), may hold values from 0 to 1
- fading_left_factor: bfloat16 [2048, 96], P('head'), may hold values from -0.125 to 0.125
- fading_right_factor: bfloat16 [96, 2048], P(None, 'head'), may hold values from -0.625 to 0.625
- fading_offset: float32 [2048], P('head'), may hold values from -6 to 1
- learning_speed_left: bfloat16 [2048, 96], P('head'), may hold values from -0.125 to 0.125
- learning_speed_right: bfloat16 [96, 2048], P(None, 'head'), may hold values from -0.625 to 0.625
- learning_speed_offset: float32 [2048], P('head'), may hold values from -2 to 2
- erasing_lookup_factor: float32 [2048], P('head'), may hold values from 0.1 to 1.9
- written_lookup_factor: float32 [2048], P('head'), may hold values from 0 to 1
- present_reward_factors: float32 [2048], P('head'), may hold values from -3 to 3
- lane_standard_factor: float32 [2048], P('head'), may hold values from 0.1 to 1.9
- lane_standard_offset: float32 [2048], P('head'), may hold values from -2 to 2
- caller_memory_directory: int32 [1024, 32, 2], P(None, 'head'), may hold values from 0 to 16383, as said below
- kept_target_place: int32 [1024, 32, 2], P(None, 'head'), may hold values from 0 to 16383, as said below
- caller_sequence: int32 [1024], replicated, may hold values from 0 to 1023, as said below
- approved_guesses: int32 [1024], replicated, may hold values from 0 to 16
Outputs:
- temporal_blend_result: bfloat16 [1024, 16, 2048], P('blk', None, 'head')
- new_states: float32 [4, 16384, 2048], P('head', 'blk')
- new_edges: float32 [4, 16384, 32], P('head', 'blk')
Inputs may be any that keep to these rules, and one draw needn't show every extreme that they name: `caller_memory_directory`: every entry names a slot of the pool of head group h // 8; all entries of one head group are distinct and cover its 16384 slots. For the positions p of one blk index, taken through q = caller_sequence[p], exactly 1 of the slots of each head group lie on each blk index (slot // 128). `kept_target_place`: same rules as the page table: every slot of a head group is written exactly once, and one blk index's positions write exactly 1 slots of each head group on each blk index. `caller_sequence`: A permutation of the 1024 requests.
All inputs are finite; a program needn't handle non-finite values.
Results may differ from a plain program's by a relative error of at most 0.006.
Values may be sent and summed in bfloat16 or wider, within the bound.
A program may use at most 64 MiB of HBM per device.

v0:
```python
import jax
import jax.numpy as jnp
from jax import lax
from jax.sharding import PartitionSpec as P

EPSILON = 1e-05
NORM_EPSILON = 0.00064


def local(
    layer_entry_vectors,
    guessed_lookup_vectors,
    guessed_content_vectors,
    gating_query,
    lane_memory_store,
    prior_step_store,
    fading_blend_ratio,
    learning_speed_blend,
    fading_left_factor,
    fading_right_factor,
    fading_offset,
    learning_speed_left,
    learning_speed_right,
    learning_speed_offset,
    erasing_lookup_factor,
    written_lookup_factor,
    present_reward_factors,
    lane_standard_factor,
    lane_standard_offset,
    caller_memory_directory,
    kept_target_place,
    caller_sequence,
    approved_guesses,
):
    blocks = lax.axis_size("blk")
    me_block = lax.axis_index("blk")
    requests_on_device = layer_entry_vectors.shape[0]
    draft_length = layer_entry_vectors.shape[1]
    width_on_device = layer_entry_vectors.shape[2]
    heads_on_device = caller_memory_directory.shape[1]
    halves = caller_memory_directory.shape[2]
    slot_dev = lane_memory_store.shape[1]
    per_peer = slot_dev // blocks
    head_width = width_on_device // heads_on_device
    slot_rows = head_width // halves
    slot_base = me_block * slot_dev
    requests = lax.dynamic_slice_in_dim(
        caller_sequence, me_block * requests_on_device, requests_on_device
    )
    counts = approved_guesses[requests]
    wanted = caller_memory_directory[requests].reshape(slot_dev)
    targets = kept_target_place[requests].reshape(slot_dev)
    item_ids = jnp.arange(slot_dev, dtype=jnp.int32)
    fetch_sort = jnp.argsort(wanted // slot_dev * slot_dev + item_ids)
    fetch_back = jnp.argsort(fetch_sort)
    asked_for = lax.all_to_all(
        wanted[fetch_sort].reshape(blocks, per_peer), "blk", split_axis=0, concat_axis=0, tiled=True
    )
    local_slots = asked_for.reshape(slot_dev) - slot_base
    got_states, got_edges = (
        lax.all_to_all(
            lane_memory_store[0][local_slots]
            .reshape(blocks, per_peer, slot_rows * head_width)
            .astype(jnp.bfloat16),
            "blk",
            split_axis=0,
            concat_axis=0,
            tiled=True,
        ).astype(jnp.float32),
        lax.all_to_all(
            prior_step_store[0][local_slots]
            .reshape(blocks, per_peer, slot_rows)
            .astype(jnp.bfloat16),
            "blk",
            split_axis=0,
            concat_axis=0,
            tiled=True,
        ).astype(jnp.float32),
    )
    recept_rows = lax.all_to_all(gating_query, "head", split_axis=2, concat_axis=1, tiled=True)
    current = layer_entry_vectors.astype(jnp.float32)
    row_count = requests_on_device * draft_length
    edge_first = got_edges.reshape(slot_dev, slot_rows)[fetch_back].reshape(
        requests_on_device, width_on_device
    )
    previous = jnp.concatenate([edge_first[:, None, :], current[:, :-1]], axis=1)
    shift_delta = previous - current
    mixed_decay = (
        (current + shift_delta * fading_blend_ratio)
        .astype(jnp.bfloat16)
        .reshape(row_count, width_on_device)
    )
    mixed_rate = (
        (current + shift_delta * learning_speed_blend)
        .astype(jnp.bfloat16)
        .reshape(row_count, width_on_device)
    )
    partial_terms = jnp.concatenate(
        [
            jnp.dot(mixed_decay, fading_left_factor, preferred_element_type=jnp.float32),
            jnp.dot(mixed_rate, learning_speed_left, preferred_element_type=jnp.float32),
        ],
        axis=1,
    )
    summed_rows = lax.psum(partial_terms.astype(jnp.bfloat16), "head").astype(jnp.float32)
    low_rank_weight = fading_left_factor.shape[1]
    decay_inner = jnp.tanh(summed_rows[:, :low_rank_weight]).astype(jnp.bfloat16)
    rate_inner = summed_rows[:, low_rank_weight:].astype(jnp.bfloat16)
    decay_term = jnp.dot(
        decay_inner, fading_right_factor, preferred_element_type=jnp.float32
    ).reshape(requests_on_device, draft_length, width_on_device)
    rate_term = jnp.dot(
        rate_inner, learning_speed_right, preferred_element_type=jnp.float32
    ).reshape(requests_on_device, draft_length, width_on_device)
    forget = jnp.exp(-jnp.exp(-jax.nn.softplus(-(fading_offset + decay_term)) - 0.5))
    in_rate = jax.nn.sigmoid(learning_speed_offset + rate_term)
    key_full = guessed_lookup_vectors.astype(jnp.float32)
    grouped = (key_full * erasing_lookup_factor).reshape(
        requests_on_device, draft_length, heads_on_device, head_width
    )
    unit_key = grouped * lax.rsqrt(jnp.sum(grouped * grouped, axis=-1, keepdims=True) + EPSILON)
    adjusted_lookup = key_full * (1.0 + (in_rate - 1.0) * written_lookup_factor)
    content_lines = guessed_content_vectors.astype(jnp.float32)
    gating_query_lines = recept_rows.astype(jnp.float32)
    start_states = got_states.reshape(slot_dev, slot_rows * head_width)[fetch_back].reshape(
        requests_on_device, heads_on_device, head_width, head_width
    )

    def by_step(array):
        return jnp.moveaxis(
            array.reshape(requests_on_device, draft_length, heads_on_device, head_width), 1, 0
        )

    def advance(carried, per_step):
        carry_state, accepted_state = carried
        step_index, forget_t, unit_t, rate_t, key_t, value_t, recept_t = per_step
        projected = jnp.sum(carry_state * unit_t[:, :, None, :], axis=-1)
        carry_state = (
            carry_state * forget_t[:, :, None, :]
            - projected[..., None] * (rate_t * unit_t)[:, :, None, :]
            + value_t[..., None] * key_t[:, :, None, :]
        )
        output = jnp.sum(carry_state * recept_t[:, :, None, :], axis=-1)
        accepted_state = jnp.where(
            (counts == step_index + 1)[:, None, None, None], carry_state, accepted_state
        )
        return ((carry_state, accepted_state), output)

    step_ids = jnp.arange(draft_length, dtype=jnp.int32)
    carried, outputs = lax.scan(
        advance,
        (start_states, start_states),
        (
            step_ids,
            by_step(forget),
            by_step(unit_key),
            by_step(in_rate),
            by_step(adjusted_lookup),
            by_step(content_lines),
            by_step(gating_query_lines),
        ),
    )
    outputs = jnp.moveaxis(outputs, 0, 1)
    average = jnp.mean(outputs, axis=-1, keepdims=True)
    centered = outputs - average
    variance = jnp.mean(centered * centered, axis=-1, keepdims=True)
    standardized_lines = centered * lax.rsqrt(
        variance + NORM_EPSILON
    ) * lane_standard_factor.reshape(heads_on_device, head_width) + lane_standard_offset.reshape(
        heads_on_device, head_width
    )
    present_reward_term = jnp.sum(
        (gating_query_lines * adjusted_lookup * present_reward_factors).reshape(
            requests_on_device, draft_length, heads_on_device, head_width
        ),
        axis=-1,
        keepdims=True,
    ) * content_lines.reshape(requests_on_device, draft_length, heads_on_device, head_width)
    temporal_blend_result = (
        (standardized_lines + present_reward_term)
        .astype(jnp.bfloat16)
        .reshape(requests_on_device, draft_length, width_on_device)
    )
    last_token = jnp.maximum(counts - 1, 0)
    picked = jnp.take_along_axis(current, last_token[:, None, None], axis=1)[:, 0]
    new_edge_rows = jnp.where((counts > 0)[:, None], picked, edge_first)
    return_sort = jnp.argsort(targets // slot_dev * slot_dev + item_ids)
    send_states = (
        carried[1]
        .reshape(slot_dev, slot_rows * head_width)[return_sort]
        .reshape(blocks, per_peer, slot_rows * head_width)
    )
    send_edges = new_edge_rows.reshape(slot_dev, slot_rows)[return_sort].reshape(
        blocks, per_peer, slot_rows
    )
    back_states, back_edges, back_slots = (
        lax.all_to_all(send_states, "blk", split_axis=0, concat_axis=0, tiled=True),
        lax.all_to_all(send_edges, "blk", split_axis=0, concat_axis=0, tiled=True),
        lax.all_to_all(
            targets[return_sort].reshape(blocks, per_peer),
            "blk",
            split_axis=0,
            concat_axis=0,
            tiled=True,
        ),
    )
    placing = jnp.argsort(back_slots.reshape(slot_dev) - slot_base)
    new_states = back_states.reshape(slot_dev, slot_rows * head_width)[placing][None]
    new_edges = back_edges.reshape(slot_dev, slot_rows)[placing][None]
    return (temporal_blend_result, new_states, new_edges)


def solution(mesh):
    return jax.shard_map(
        local,
        mesh=mesh,
        in_specs=(
            P("blk", None, "head"),
            P("blk", None, "head"),
            P("blk", None, "head"),
            P("blk", "head", None),
            P("head", "blk", None),
            P("head", "blk", None),
            P("head"),
            P("head"),
            P("head", None),
            P(None, "head"),
            P("head"),
            P("head", None),
            P(None, "head"),
            P("head"),
            P("head"),
            P("head"),
            P("head"),
            P("head"),
            P("head"),
            P(None, "head", None),
            P(None, "head", None),
            P(),
            P(),
        ),
        out_specs=(P("blk", None, "head"), P("head", "blk", None), P("head", "blk", None)),
        check_vma=False,
    )
```

profile of v0, /device:TPU:1, one launch (start us, length us, event | category | flops | bytes accessed | tf_op | source)
XLA Modules:
  0.0 456.3 jit_solution(10310491312768737834)
XLA Ops:
  8.2 18.4 %all-to-all-start = ((s32[128,1,1]{2,1,0:T(1,128)}), s32[128,1,1]{2,1,0:T(1,128)S(1)}, u32[]{:S(2)}, u32[]{:S(2)}) async-start(s32[128,1,1]{2,1,0:T(1,128)} %copy.106), calls=%async_computation | async-start | bytes 131072 | tf_op jit(solution)/shard_map/all_to_all | solution.py:56
  38.0 12.1 %all-to-all-start.5 = ((s32[128,1,1]{2,1,0:T(1,128)}), s32[128,1,1]{2,1,0:T(1,128)S(1)}, u32[]{:S(2)}, u32[]{:S(2)}) async-start(s32[128,1,1]{2,1,0:T(1,128)} %copy.126), calls=%async_computation.5 | async-start | bytes 131072 | tf_op jit(solution)/shard_map/all_to_all | solution.py:199
  50.2 11.2 %all-to-all-done.5 = s32[128,1,1]{2,1,0:T(1,128)S(1)} async-done(((s32[128,1,1]{2,1,0:T(1,128)}), s32[128,1,1]{2,1,0:T(1,128)S(1)}, u32[]{:S(2)}, u32[]{:S(2)}) %all-to-all-start.5) | async-done | bytes 544 | tf_op jit(solution)/shard_map/all_to_all | solution.py:199
  61.5 5.0 %subtract_reduce_fusion = (s32[128]{0:T(128)}, s32[128]{0:T(128)S(1)}) fusion(s32[128,1,1]{2,1,0:T(1,128)S(1)} %all-to-all-done.5, s32[]{:T(128)S(6)} %mul.167, s32[128,1,1]{2,1,0:T(1,128)S(1)} %all-to-all-done), kind=kLoop, calls=%fused_computation.63 | loop fusion | flops 256 | bytes 2052 | tf_op jit(solution)/shard_map/sub | solution.py:207
  67.9 6.7 %all-to-all-start.2 = ((bf16[128,1,32]{2,1,0:T(2,128)(2,1)}), bf16[128,1,32]{2,1,0:T(2,128)(2,1)}, u32[]{:S(2)}, u32[]{:S(2)}) async-start(bf16[128,1,32]{2,1,0:T(2,128)(2,1)} %copy.110), calls=%async_computation.2 | async-start | bytes 131072 | tf_op jit(solution)/shard_map/all_to_all | solution.py:70
  89.3 4.0 all-to-all-start.3
  95.7 13.9 %psum.7 = bf16[128,192]{0,1:T(8,128)(2,1)S(1)} all-reduce(bf16[128,192]{0,1:T(8,128)(2,1)S(1)} %pad_maximum_fusion), channel_id=1, replica_groups=mesh['blk'=128,'head'=4] {'head'}, use_global_device_ids=true, to_apply=%region_2.3 | all-reduce | flops 24576 | bytes 98304 | tf_op jit(solution)/shard_map/psum | solution.py:105
  114.6 18.6 %all-to-all-start.1 = ((bf16[128,2,1024]{2,1,0:T(2,128)(2,1)}), bf16[128,2,1024]{2,1,0:T(2,128)(2,1)}, u32[]{:S(2)}, u32[]{:S(2)}) async-start(bf16[128,2,1024]{2,1,0:T(2,128)(2,1)} %reshape.397), calls=%async_computation.1 | async-start | bytes 1048576 | tf_op jit(solution)/shard_map/all_to_all | solution.py:61
  133.2 3.3 reshape.400
  138.7 3.5 copy.120
  142.2 3.5 copy.119
  153.4 10.6 %all-to-all-start.6 = ((f32[128,1,32]{2,1,0:T(1,128)}), f32[128,1,32]{2,1,0:T(1,128)S(1)}, u32[]{:S(2)}, u32[]{:S(2)}) async-start(f32[128,1,32]{2,1,0:T(1,128)} %bitcast.36), calls=%async_computation.6 | async-start | bytes 131072 | tf_op jit(solution)/shard_map/all_to_all | solution.py:198
  164.0 3.6 reshape.398
  173.4 230.6 %while.14 = (s32[]{:T(128)}, f32[8,8,64,64]{3,2,1,0:T(8,128)S(1)}, f32[8,8,64,64]{3,2,1,0:T(8,128)}, f32[16,8,8,64]{3,2,1,0:T(8,128)}, f32[16,8,8,64]{3,2,1,0:T(...) while((s32[]{:T(128)}, f32[8,8,64,64]{3,2,1,0:T(8,128)S(1)}, ...), condition=%wide.region_7.8_spmd, body=%wide.region_4.7_spmd.sunk | while | flops 2363466 | bytes 15057189 | solution.py:150
  178.0 8.4 %multiply_reduce_fusion.5 = (f32[8,8,64]{2,1,0:T(8,128)S(1)}, f32[8,8,64,64]{3,2,1,0:T(8,128)S(1)}, f32[8,8,64,64]{3,2,1,0:T(8,128)S(1)}) fusion(f32[8,8,64]{2,1,0:T(8,128)S(1)} %get-tuple-element.211, f32[8,8,64,64]{3,2,1,0:T(8,128)S(1)} %copy-done.1, pred[8]{0:T(512)(128)(4,1)S(1)} %broadcast_compare_fusion.4, ...), kind=kOutput, calls=%fused_computation.15.clone.1 | output fusion | flops 2359359 | bytes 4309000 | tf_op jit(solution)/shard_map/while/body/eval_jaxpr/mul | solution.py:140
  192.4 8.4 %multiply_reduce_fusion.5 = (f32[8,8,64]{2,1,0:T(8,128)S(1)}, f32[8,8,64,64]{3,2,1,0:T(8,128)S(1)}, f32[8,8,64,64]{3,2,1,0:T(8,128)S(1)}) fusion(f32[8,8,64]{2,1,0:T(8,128)S(1)} %get-tuple-element.211, f32[8,8,64,64]{3,2,1,0:T(8,128)S(1)} %copy-done.1, pred[8]{0:T(512)(128)(4,1)S(1)} %broadcast_compare_fusion.4, ...), kind=kOutput, calls=%fused_computation.15.clone.1 | output fusion | flops 2359359 | bytes 4309000 | tf_op jit(solution)/shard_map/while/body/eval_jaxpr/mul | solution.py:140
  206.9 8.4 %multiply_reduce_fusion.5 = (f32[8,8,64]{2,1,0:T(8,128)S(1)}, f32[8,8,64,64]{3,2,1,0:T(8,128)S(1)}, f32[8,8,64,64]{3,2,1,0:T(8,128)S(1)}) fusion(f32[8,8,64]{2,1,0:T(8,128)S(1)} %get-tuple-element.211, f32[8,8,64,64]{3,2,1,0:T(8,128)S(1)} %copy-done.1, pred[8]{0:T(512)(128)(4,1)S(1)} %broadcast_compare_fusion.4, ...), kind=kOutput, calls=%fused_computation.15.clone.1 | output fusion | flops 2359359 | bytes 4309000 | tf_op jit(solution)/shard_map/while/body/eval_jaxpr/mul | solution.py:140
  221.3 8.4 %multiply_reduce_fusion.5 = (f32[8,8,64]{2,1,0:T(8,128)S(1)}, f32[8,8,64,64]{3,2,1,0:T(8,128)S(1)}, f32[8,8,64,64]{3,2,1,0:T(8,128)S(1)}) fusion(f32[8,8,64]{2,1,0:T(8,128)S(1)} %get-tuple-element.211, f32[8,8,64,64]{3,2,1,0:T(8,128)S(1)} %copy-done.1, pred[8]{0:T(512)(128)(4,1)S(1)} %broadcast_compare_fusion.4, ...), kind=kOutput, calls=%fused_computation.15.clone.1 | output fusion | flops 2359359 | bytes 4309000 | tf_op jit(solution)/shard_map/while/body/eval_jaxpr/mul | solution.py:140
  235.7 8.4 %multiply_reduce_fusion.5 = (f32[8,8,64]{2,1,0:T(8,128)S(1)}, f32[8,8,64,64]{3,2,1,0:T(8,128)S(1)}, f32[8,8,64,64]{3,2,1,0:T(8,128)S(1)}) fusion(f32[8,8,64]{2,1,0:T(8,128)S(1)} %get-tuple-element.211, f32[8,8,64,64]{3,2,1,0:T(8,128)S(1)} %copy-done.1, pred[8]{0:T(512)(128)(4,1)S(1)} %broadcast_compare_fusion.4, ...), kind=kOutput, calls=%fused_computation.15.clone.1 | output fusion | flops 2359359 | bytes 4309000 | tf_op jit(solution)/shard_map/while/body/eval_jaxpr/mul | solution.py:140
  250.1 8.4 %multiply_reduce_fusion.5 = (f32[8,8,64]{2,1,0:T(8,128)S(1)}, f32[8,8,64,64]{3,2,1,0:T(8,128)S(1)}, f32[8,8,64,64]{3,2,1,0:T(8,128)S(1)}) fusion(f32[8,8,64]{2,1,0:T(8,128)S(1)} %get-tuple-element.211, f32[8,8,64,64]{3,2,1,0:T(8,128)S(1)} %copy-done.1, pred[8]{0:T(512)(128)(4,1)S(1)} %broadcast_compare_fusion.4, ...), kind=kOutput, calls=%fused_computation.15.clone.1 | output fusion | flops 2359359 | bytes 4309000 | tf_op jit(solution)/shard_map/while/body/eval_jaxpr/mul | solution.py:140
  264.5 8.4 %multiply_reduce_fusion.5 = (f32[8,8,64]{2,1,0:T(8,128)S(1)}, f32[8,8,64,64]{3,2,1,0:T(8,128)S(1)}, f32[8,8,64,64]{3,2,1,0:T(8,128)S(1)}) fusion(f32[8,8,64]{2,1,0:T(8,128)S(1)} %get-tuple-element.211, f32[8,8,64,64]{3,2,1,0:T(8,128)S(1)} %copy-done.1, pred[8]{0:T(512)(128)(4,1)S(1)} %broadcast_compare_fusion.4, ...), kind=kOutput, calls=%fused_computation.15.clone.1 | output fusion | flops 2359359 | bytes 4309000 | tf_op jit(solution)/shard_map/while/body/eval_jaxpr/mul | solution.py:140
  278.9 8.4 %multiply_reduce_fusion.5 = (f32[8,8,64]{2,1,0:T(8,128)S(1)}, f32[8,8,64,64]{3,2,1,0:T(8,128)S(1)}, f32[8,8,64,64]{3,2,1,0:T(8,128)S(1)}) fusion(f32[8,8,64]{2,1,0:T(8,128)S(1)} %get-tuple-element.211, f32[8,8,64,64]{3,2,1,0:T(8,128)S(1)} %copy-done.1, pred[8]{0:T(512)(128)(4,1)S(1)} %broadcast_compare_fusion.4, ...), kind=kOutput, calls=%fused_computation.15.clone.1 | output fusion | flops 2359359 | bytes 4309000 | tf_op jit(solution)/shard_map/while/body/eval_jaxpr/mul | solution.py:140
  293.3 8.4 %multiply_reduce_fusion.5 = (f32[8,8,64]{2,1,0:T(8,128)S(1)}, f32[8,8,64,64]{3,2,1,0:T(8,128)S(1)}, f32[8,8,64,64]{3,2,1,0:T(8,128)S(1)}) fusion(f32[8,8,64]{2,1,0:T(8,128)S(1)} %get-tuple-element.211, f32[8,8,64,64]{3,2,1,0:T(8,128)S(1)} %copy-done.1, pred[8]{0:T(512)(128)(4,1)S(1)} %broadcast_compare_fusion.4, ...), kind=kOutput, calls=%fused_computation.15.clone.1 | output fusion | flops 2359359 | bytes 4309000 | tf_op jit(solution)/shard_map/while/body/eval_jaxpr/mul | solution.py:140
  307.7 8.4 %multiply_reduce_fusion.5 = (f32[8,8,64]{2,1,0:T(8,128)S(1)}, f32[8,8,64,64]{3,2,1,0:T(8,128)S(1)}, f32[8,8,64,64]{3,2,1,0:T(8,128)S(1)}) fusion(f32[8,8,64]{2,1,0:T(8,128)S(1)} %get-tuple-element.211, f32[8,8,64,64]{3,2,1,0:T(8,128)S(1)} %copy-done.1, pred[8]{0:T(512)(128)(4,1)S(1)} %broadcast_compare_fusion.4, ...), kind=kOutput, calls=%fused_computation.15.clone.1 | output fusion | flops 2359359 | bytes 4309000 | tf_op jit(solution)/shard_map/while/body/eval_jaxpr/mul | solution.py:140
  322.1 8.4 %multiply_reduce_fusion.5 = (f32[8,8,64]{2,1,0:T(8,128)S(1)}, f32[8,8,64,64]{3,2,1,0:T(8,128)S(1)}, f32[8,8,64,64]{3,2,1,0:T(8,128)S(1)}) fusion(f32[8,8,64]{2,1,0:T(8,128)S(1)} %get-tuple-element.211, f32[8,8,64,64]{3,2,1,0:T(8,128)S(1)} %copy-done.1, pred[8]{0:T(512)(128)(4,1)S(1)} %broadcast_compare_fusion.4, ...), kind=kOutput, calls=%fused_computation.15.clone.1 | output fusion | flops 2359359 | bytes 4309000 | tf_op jit(solution)/shard_map/while/body/eval_jaxpr/mul | solution.py:140
  336.6 8.4 %multiply_reduce_fusion.5 = (f32[8,8,64]{2,1,0:T(8,128)S(1)}, f32[8,8,64,64]{3,2,1,0:T(8,128)S(1)}, f32[8,8,64,64]{3,2,1,0:T(8,128)S(1)}) fusion(f32[8,8,64]{2,1,0:T(8,128)S(1)} %get-tuple-element.211, f32[8,8,64,64]{3,2,1,0:T(8,128)S(1)} %copy-done.1, pred[8]{0:T(512)(128)(4,1)S(1)} %broadcast_compare_fusion.4, ...), kind=kOutput, calls=%fused_computation.15.clone.1 | output fusion | flops 2359359 | bytes 4309000 | tf_op jit(solution)/shard_map/while/body/eval_jaxpr/mul | solution.py:140
  351.0 8.4 %multiply_reduce_fusion.5 = (f32[8,8,64]{2,1,0:T(8,128)S(1)}, f32[8,8,64,64]{3,2,1,0:T(8,128)S(1)}, f32[8,8,64,64]{3,2,1,0:T(8,128)S(1)}) fusion(f32[8,8,64]{2,1,0:T(8,128)S(1)} %get-tuple-element.211, f32[8,8,64,64]{3,2,1,0:T(8,128)S(1)} %copy-done.1, pred[8]{0:T(512)(128)(4,1)S(1)} %broadcast_compare_fusion.4, ...), kind=kOutput, calls=%fused_computation.15.clone.1 | output fusion | flops 2359359 | bytes 4309000 | tf_op jit(solution)/shard_map/while/body/eval_jaxpr/mul | solution.py:140
  365.4 8.4 %multiply_reduce_fusion.5 = (f32[8,8,64]{2,1,0:T(8,128)S(1)}, f32[8,8,64,64]{3,2,1,0:T(8,128)S(1)}, f32[8,8,64,64]{3,2,1,0:T(8,128)S(1)}) fusion(f32[8,8,64]{2,1,0:T(8,128)S(1)} %get-tuple-element.211, f32[8,8,64,64]{3,2,1,0:T(8,128)S(1)} %copy-done.1, pred[8]{0:T(512)(128)(4,1)S(1)} %broadcast_compare_fusion.4, ...), kind=kOutput, calls=%fused_computation.15.clone.1 | output fusion | flops 2359359 | bytes 4309000 | tf_op jit(solution)/shard_map/while/body/eval_jaxpr/mul | solution.py:140
  379.8 8.4 %multiply_reduce_fusion.5 = (f32[8,8,64]{2,1,0:T(8,128)S(1)}, f32[8,8,64,64]{3,2,1,0:T(8,128)S(1)}, f32[8,8,64,64]{3,2,1,0:T(8,128)S(1)}) fusion(f32[8,8,64]{2,1,0:T(8,128)S(1)} %get-tuple-element.211, f32[8,8,64,64]{3,2,1,0:T(8,128)S(1)} %copy-done.1, pred[8]{0:T(512)(128)(4,1)S(1)} %broadcast_compare_fusion.4, ...), kind=kOutput, calls=%fused_computation.15.clone.1 | output fusion | flops 2359359 | bytes 4309000 | tf_op jit(solution)/shard_map/while/body/eval_jaxpr/mul | solution.py:140
  394.2 8.4 %multiply_reduce_fusion.5 = (f32[8,8,64]{2,1,0:T(8,128)S(1)}, f32[8,8,64,64]{3,2,1,0:T(8,128)S(1)}, f32[8,8,64,64]{3,2,1,0:T(8,128)S(1)}) fusion(f32[8,8,64]{2,1,0:T(8,128)S(1)} %get-tuple-element.211, f32[8,8,64,64]{3,2,1,0:T(8,128)S(1)} %copy-done.1, pred[8]{0:T(512)(128)(4,1)S(1)} %broadcast_compare_fusion.4, ...), kind=kOutput, calls=%fused_computation.15.clone.1 | output fusion | flops 2359359 | bytes 4309000 | tf_op jit(solution)/shard_map/while/body/eval_jaxpr/mul | solution.py:140
  409.3 13.9 %all-to-all-start.4 = ((f32[128,1,2048]{2,1,0:T(1,128)}), f32[128,1,2048]{2,1,0:T(1,128)S(1)}, u32[]{:S(2)}, u32[]{:S(2)}) async-start(f32[128,1,2048]{2,1,0:T(1,128)} %copy.125), calls=%async_computation.4 | async-start | bytes 2097152 | tf_op jit(solution)/shard_map/all_to_all | solution.py:197
  432.5 21.5 %all-to-all-done.4 = f32[128,1,2048]{2,1,0:T(1,128)S(1)} async-done(((f32[128,1,2048]{2,1,0:T(1,128)}), f32[128,1,2048]{2,1,0:T(1,128)S(1)}, u32[]{:S(2)}, u32[]{:S(2)}) %all-to-all-start.4) | async-done | bytes 1048608 | tf_op jit(solution)/shard_map/all_to_all | solution.py:197
  (375 shorter events, 159.5 us)
Async XLA Ops:
  0.6 84.8 %copy-start = (f32[1,128,2048]{2,1,0:T(8,128)S(1)}, f32[1,128,2048]{2,1,0:T(8,128)}, u32[]{:S(2)}) copy-start(f32[1,128,2048]{2,1,0:T(8,128)} %param.29) | copy-start | bytes 3145732
  0.6 26.0 %copy-start.3 = (s32[1024]{0:T(1024)S(1)}, s32[1024]{0:T(1024)}, u32[]{:S(2)}) copy-start(s32[1024]{0:T(1024)} %param.47) | copy-start | bytes 12292
  0.7 27.2 %copy-start.15 = (s32[1024,8,2]{0,2,1:T(2,128)S(1)}, s32[1024,8,2]{0,2,1:T(2,128)}, u32[]{:S(2)}) copy-start(s32[1024,8,2]{0,2,1:T(2,128)} %param.45) | copy-start | bytes 196612
  1.5 48.6 %copy-start.18 = (f32[1,128,32]{1,2,0:T(8,128)S(1)}, f32[1,128,32]{1,2,0:T(8,128)}, u32[]{:S(2)}) copy-start(f32[1,128,32]{1,2,0:T(8,128)} %param.30) | copy-start | bytes 49156
  2.8 72.4 %copy-start.5 = (bf16[8,16,512]{2,1,0:T(8,128)(2,1)S(1)}, bf16[8,16,512]{2,1,0:T(8,128)(2,1)}, u32[]{:S(2)}) copy-start(bf16[8,16,512]{2,1,0:T(8,128)(2,1)} %param.25) | copy-start | bytes 393220
  8.2 29.8 %all-to-all-start = ((s32[128,1,1]{2,1,0:T(1,128)}), s32[128,1,1]{2,1,0:T(1,128)S(1)}, u32[]{:S(2)}, u32[]{:S(2)}) async-start(s32[128,1,1]{2,1,0:T(1,128)} %copy.106), calls=%async_computation | async-start | bytes 131072 | tf_op jit(solution)/shard_map/all_to_all | solution.py:56
  26.6 49.3 %copy-start.28 = (f32[512]{0:T(512)S(1)}, f32[512]{0:T(512)}, u32[]{:S(2)}) copy-start(f32[512]{0:T(512)} %param.35) | copy-start | bytes 6148
  26.7 50.0 %copy-start.19 = (f32[512]{0:T(512)S(1)}, f32[512]{0:T(512)}, u32[]{:S(2)}) copy-start(f32[512]{0:T(512)} %param.38) | copy-start | bytes 6148
  26.7 50.8 %copy-start.9 = (bf16[8,16,512]{2,1,0:T(8,128)(2,1)S(1)}, bf16[8,16,512]{2,1,0:T(8,128)(2,1)}, u32[]{:S(2)}) copy-start(bf16[8,16,512]{2,1,0:T(8,128)(2,1)} %param.27) | copy-start | bytes 393220
  31.8 34.7 %copy-start.21 = (s32[1024]{0:T(1024)}, s32[1024]{0:T(1024)S(1)}, u32[]{:S(2)}) copy-start(s32[1024]{0:T(1024)S(1)} %pad_clamp_fusion.1) | copy-start | bytes 12292
  38.0 23.5 %all-to-all-start.5 = ((s32[128,1,1]{2,1,0:T(1,128)}), s32[128,1,1]{2,1,0:T(1,128)S(1)}, u32[]{:S(2)}, u32[]{:S(2)}) async-start(s32[128,1,1]{2,1,0:T(1,128)} %copy.126), calls=%async_computation.5 | async-start | bytes 131072 | tf_op jit(solution)/shard_map/all_to_all | solution.py:199
  66.5 12.5 %copy-start.22 = (s32[1024]{0:T(1024)}, s32[1024]{0:T(1024)S(1)}, u32[]{:S(2)}) copy-start(s32[1024]{0:T(1024)S(1)} %pad_clamp_fusion.3) | copy-start | bytes 12292
  67.9 21.4 %all-to-all-start.2 = ((bf16[128,1,32]{2,1,0:T(2,128)(2,1)}), bf16[128,1,32]{2,1,0:T(2,128)(2,1)}, u32[]{:S(2)}, u32[]{:S(2)}) async-start(bf16[128,1,32]{2,1,0:T(2,128)(2,1)} %copy.110), calls=%async_computation.2 | async-start | bytes 131072 | tf_op jit(solution)/shard_map/all_to_all | solution.py:70
  86.6 8.6 %copy-start.23 = (f32[512]{0:T(512)S(1)}, f32[512]{0:T(512)}, u32[]{:S(2)}) copy-start(f32[512]{0:T(512)} %param.31) | copy-start | bytes 6148
  86.6 8.6 %copy-start.24 = (f32[512]{0:T(512)S(1)}, f32[512]{0:T(512)}, u32[]{:S(2)}) copy-start(f32[512]{0:T(512)} %param.32) | copy-start | bytes 6148
  86.6 8.8 %copy-start.11 = (bf16[512,96]{0,1:T(8,128)(2,1)S(1)}, bf16[512,96]{0,1:T(8,128)(2,1)}, u32[]{:S(2)}) copy-start(bf16[512,96]{0,1:T(8,128)(2,1)} %param.33) | copy-start | bytes 294916
  86.6 8.9 %copy-start.12 = (bf16[512,96]{0,1:T(8,128)(2,1)S(1)}, bf16[512,96]{0,1:T(8,128)(2,1)}, u32[]{:S(2)}) copy-start(bf16[512,96]{0,1:T(8,128)(2,1)} %param.36) | copy-start | bytes 294916
  87.1 22.5 %copy-start.13 = (bf16[96,512]{1,0:T(8,128)(2,1)S(1)}, bf16[96,512]{1,0:T(8,128)(2,1)}, u32[]{:S(2)}) copy-start(bf16[96,512]{1,0:T(8,128)(2,1)} %param.37) | copy-start | bytes 294916
  88.1 21.7 %copy-start.14 = (bf16[96,512]{1,0:T(8,128)(2,1)S(1)}, bf16[96,512]{1,0:T(8,128)(2,1)}, u32[]{:S(2)}) copy-start(bf16[96,512]{1,0:T(8,128)(2,1)} %param.34) | copy-start | bytes 294916
  89.3 24.7 %all-to-all-start.3 = ((bf16[4,2,8192]{2,1,0:T(2,128)(2,1)}), bf16[4,2,8192]{2,1,0:T(2,128)(2,1)S(1)}, u32[]{:S(2)}, u32[]{:S(2)}) async-start(bf16[4,2,8192]{2,1,0:T(2,128)(2,1)} %reshape.399), calls=%async_computation.3 | async-start | bytes 262144 | tf_op jit(solution)/shard_map/all_to_all | solution.py:80
  94.2 16.1 %copy-start.17 = (f32[8,64]{1,0:T(8,128)S(1)}, f32[8,64]{1,0:T(8,128)}, u32[]{:S(2)}) copy-start(f32[8,64]{1,0:T(8,128)} %add.166) | copy-start | bytes 6148
  95.3 16.3 %copy-start.16 = (f32[8,64]{1,0:T(8,128)S(1)}, f32[8,64]{1,0:T(8,128)}, u32[]{:S(2)}) copy-start(f32[8,64]{1,0:T(8,128)} %add.174) | copy-start | bytes 6148
  114.6 38.8 %all-to-all-start.1 = ((bf16[128,2,1024]{2,1,0:T(2,128)(2,1)}), bf16[128,2,1024]{2,1,0:T(2,128)(2,1)}, u32[]{:S(2)}, u32[]{:S(2)}) async-start(bf16[128,2,1024]{2,1,0:T(2,128)(2,1)} %reshape.397), calls=%async_computation.1 | async-start | bytes 1048576 | tf_op jit(solution)/shard_map/all_to_all | solution.py:61
  142.2 4.6 %copy-start.10 = (bf16[8,16,512]{2,1,0:T(8,128)(2,1)S(1)}, bf16[8,16,512]{2,1,0:T(8,128)(2,1)}, u32[]{:S(2)}) copy-start(bf16[8,16,512]{2,1,0:T(8,128)(2,1)} %param.26) | copy-start | bytes 393220
  142.2 4.6 %copy-start.20 = (f32[512]{0:T(512)S(1)}, f32[512]{0:T(512)}, u32[]{:S(2)}) copy-start(f32[512]{0:T(512)} %param.38) | copy-start | bytes 6148
  153.4 255.8 %all-to-all-start.6 = ((f32[128,1,32]{2,1,0:T(1,128)}), f32[128,1,32]{2,1,0:T(1,128)S(1)}, u32[]{:S(2)}, u32[]{:S(2)}) async-start(f32[128,1,32]{2,1,0:T(1,128)} %bitcast.36), calls=%async_computation.6 | async-start | bytes 131072 | tf_op jit(solution)/shard_map/all_to_all | solution.py:198
  407.2 16.0 %copy-start.29 = (f32[512]{0:T(512)S(1)}, f32[512]{0:T(512)}, u32[]{:S(2)}) copy-start(f32[512]{0:T(512)} %param.42) | copy-start | bytes 6148
  407.2 16.0 %copy-start.30 = (f32[512]{0:T(512)S(1)}, f32[512]{0:T(512)}, u32[]{:S(2)}) copy-start(f32[512]{0:T(512)} %param.43) | copy-start | bytes 6148
  407.2 16.1 %copy-start.31 = (s32[128]{0:T(128)S(1)}, s32[128]{0:T(128)}, u32[]{:S(2)}) copy-start(s32[128]{0:T(128)} %get-tuple-element.129) | copy-start | bytes 1540
  407.2 20.0 %copy-start.6 = (f32[8,16,512]{2,1,0:T(8,128)S(1)}, f32[8,16,512]{2,1,0:T(8,128)}, u32[]{:S(2)}) copy-start(f32[8,16,512]{2,1,0:T(8,128)} %get-tuple-element.115) | copy-start | bytes 786436
  409.3 20.2 %copy-start.4 = (f32[16,8,8,64]{3,2,1,0:T(8,128)S(1)}, f32[16,8,8,64]{3,2,1,0:T(8,128)}, u32[]{:S(2)}) copy-start(f32[16,8,8,64]{3,2,1,0:T(8,128)} %get-tuple-element.72) | copy-start | bytes 786436
  409.3 44.8 %all-to-all-start.4 = ((f32[128,1,2048]{2,1,0:T(1,128)}), f32[128,1,2048]{2,1,0:T(1,128)S(1)}, u32[]{:S(2)}, u32[]{:S(2)}) async-start(f32[128,1,2048]{2,1,0:T(1,128)} %copy.125), calls=%async_computation.4 | async-start | bytes 2097152 | tf_op jit(solution)/shard_map/all_to_all | solution.py:197
  (40 other events, 97.7 us)
where the time goes:
time: 461 us; the launch traced here: 456 us
  other arithmetic  178 us (39%)
  local copies, waits for them, and re-layouts  129 us (28%)
  starting transfers between devices  84.2 us (18%)
  waiting for transfers between devices  37.6 us (8%)
  blocking collectives  13.9 us (3%)
  loops' own time  11.1 us (2%)
    mul x16, other arithmetic, advance(): projected[..., None] * (rate_t * unit_t)[:, :, None, :]  135 us
    all_to_all x1, waiting for transfers between devices, local(): lax.all_to_all(send_states, 'blk', split_axis=0, concat_axis=0, tiled=True)  21.5 us
    unnamed x78, local copies, waits for them, and re-layouts  19.3 us
    all_to_all x1, starting transfers between devices, local(): lax.all_to_all(lane_memory_store[0][local_slots].reshape(blocks, per_peer...  18.6 us
    all_to_all x1, starting transfers between devices, local(): lax.all_to_all(wanted[fetch_sort].reshape(blocks, per_peer), 'blk', split...  18.4 us
    mul x16, other arithmetic, advance(): rate_t * unit_t  14.5 us
    psum x1, blocking collectives, local(): lax.psum(partial_terms.astype(jnp.bfloat16), 'head').astype(jnp.float32)  13.9 us
    all_to_all x1, starting transfers between devices, local(): lax.all_to_all(send_states, 'blk', split_axis=0, concat_axis=0, tiled=True)  13.9 us
  transfers between devices with their start and end apart: 7, of which 4 were waited for; matrix products, arithmetic and copies ran while one was open for 61% of the time, Pallas kernels for 0%

commit v1 on v0

v1 whole, which is shorter than its diff:
```python
import functools

import jax
import jax.numpy as jnp
from jax import lax
from jax.experimental import pallas as pl
from jax.experimental.pallas import tpu as pltpu
from jax.sharding import PartitionSpec as P

EPSILON = 1e-05
NORM_EPSILON = 0.00064
DECAY_SCALE = 0.6065306597126334

MESH = pl.DeviceIdType.MESH
F32 = jnp.float32
BF16 = jnp.bfloat16
I32 = jnp.int32

NB = 128
NH = 4
REQ = 8
STEPS = 16
WIDTH = 512
HEADS = 8
HW = 64
ROWS = 32
NC = 2
CROWS = ROWS // NC
CW = CROWS * HW
CT = CW // 128
RB = 4

NT = (((1,), (1,)), ((), ()))
TN = (((0,), (0,)), ((), ()))
NN = (((1,), (0,)), ((), ()))


def mm(a, b, dims=NN):
    return lax.dot_general(a, b, dims, preferred_element_type=F32)


def hot(mask):
    return jnp.where(mask, 1.0, 0.0).astype(BF16)


def kernel(
    x_ref, k_ref, v_ref, rq_ref, st_ref, ed_ref,
    ratio_d, ratio_r, off_d, off_r, erase, written, reward, gain, shift,
    left_d, right_d, left_r, right_r,
    dir_ref, tgt_ref, seqv_ref, seq_sm, app_sm,
    tb_ref, ns_ref, ne_ref,
    stag, recv, stag_e, recv_e, back_s, back_r, back_es, back_er,
    r_recv, pb, pr, pb0, pr0,
    hi_s, tr_s, xs, kept, st_t,
    f_r, u_r, a_r, k_r, r_r, r_s, v_r, o_r, bonus_s,
    f_t, u_t, au_t, k_t, r_t, v_t, o_t,
    ss, rs, ss_e, rs_e, ss_b, rs_b, ss_be, rs_be, ss_h, rs_h,
):
    me = lax.axis_index("blk")
    hd = lax.axis_index("head")
    z = lax.div(me, 16)
    y = lax.rem(lax.div(me, 2), 8)
    core = lax.rem(me, 2)
    z_off = [lax.rem(z + i, 8) * 16 for i in range(8)]
    y_off = [lax.rem(y + i, 8) * 2 for i in range(8)]
    c_off = [core, 1 - core]
    far = (4, 3, 5, 2, 6, 1, 7, 0)
    inner = [(b, c) for b in far for c in (1, 0)]

    barrier = pltpu.get_barrier_semaphore()
    for a in far:
        for b, c in inner:
            if a or b or c:
                pl.semaphore_signal(
                    barrier, inc=1, device_id=(z_off[a] + y_off[b] + c_off[c], hd), device_id_type=MESH
                )
    for i in range(1, NH):
        pl.semaphore_signal(barrier, inc=1, device_id=(me, lax.rem(hd + i, NH)), device_id_type=MESH)

    def to_all(src, dst, send_sem, recv_sem):
        def start(d):
            pltpu.make_async_remote_copy(
                src_ref=src.at[d], dst_ref=dst.at[me], send_sem=send_sem, recv_sem=recv_sem,
                device_id=(d, hd), device_id_type=MESH,
            ).start()

        def ring(a, carry):
            dz = 4 + lax.div(a + 1, 2) * (1 - 2 * lax.rem(a, 2))
            base = lax.rem(z + dz, 8) * 16
            for b, c in inner:
                start(base + y_off[b] + c_off[c])
            return carry

        lax.fori_loop(0, 7, ring, 0)
        for b, c in inner[:-1]:
            start(z_off[0] + y_off[b] + c_off[c])

    def all_of(src, dst, send_sem, recv_sem):
        return pltpu.make_async_remote_copy(
            src_ref=src.at[pl.ds(0, NB - 1)], dst_ref=dst.at[pl.ds(0, NB - 1)],
            send_sem=send_sem, recv_sem=recv_sem, device_id=(me, hd), device_id_type=MESH,
        )

    lane = lax.broadcasted_iota(I32, (NB, 128), 1)
    sub = lax.broadcasted_iota(I32, (NB, 128), 0)
    lane_f = lane.astype(F32)

    fetch_q = jnp.zeros((2, 1024), I32)
    place_q = jnp.zeros((2, 1024), I32)
    for h in range(HEADS):
        dv = dir_ref[h]
        tv = tgt_ref[h]
        fetch_q = fetch_q + jnp.where((dv >> 7) == me, dv & 127, 0)
        place_q = place_q + jnp.where((tv >> 7) == me, tv & 127, 0)
        hi_s[2 * h : 2 * h + 2, :] = (dv >> 7).astype(F32)
        hi_s[16 + 2 * h : 18 + 2 * h, :] = (tv >> 7).astype(F32)
    both_q = jnp.sum((fetch_q + place_q * 128).astype(F32), axis=0, keepdims=True)
    seq_t = jnp.transpose(seqv_ref[...].astype(F32))
    cols = []
    for s in range(8):
        col = jnp.broadcast_to(seq_t[:, s : s + 1], (128, 128))
        acc = jnp.zeros((128, 128), F32)
        for qt in range(8):
            acc = acc + jnp.where(
                col == lane_f + float(128 * qt), both_q[:, qt * 128 : (qt + 1) * 128], 0.0
            )
        grouped = jnp.sum(acc.reshape(16, 8, 128), axis=1)
        cols.append(jnp.sum(grouped, axis=1, keepdims=True))
    both = jnp.concatenate(cols, axis=0)
    place = jnp.floor(both * (1.0 / 128.0))
    fetch = both - 128.0 * place
    pick = hot(fetch == lane_f)
    put = hot(place == lane_f)

    row8 = lax.broadcasted_iota(I32, (REQ, 1024), 0)
    lane1024 = lax.broadcasted_iota(I32, (REQ, 1024), 1)
    q_of = jnp.zeros((REQ, 1024), I32)
    count_row = jnp.zeros((1, 128), I32)
    count_col = jnp.zeros((REQ, WIDTH), I32)
    lane1 = lax.broadcasted_iota(I32, (1, 128), 1)
    row8w = lax.broadcasted_iota(I32, (REQ, WIDTH), 0)
    for i in range(REQ):
        q = seq_sm[me * REQ + i]
        n = app_sm[q]
        q_of = jnp.where(row8 == i, q, q_of)
        count_row = jnp.where(lax.rem(lane1, 8) == i, n, count_row)
        count_col = jnp.where(row8w == i, n, count_col)
    own = jnp.where(q_of == lane1024, 1.0, 0.0)
    own = jnp.concatenate([own] * 16, axis=0).astype(BF16)
    spread = mm(hi_s[...].astype(BF16), own, NT)
    r_id = lax.broadcasted_iota(I32, (16, 128), 0)
    l_id = lax.broadcasted_iota(I32, (16, 128), 1)
    group = lax.rem(r_id, 2) * 8 + lax.rem(lax.div(r_id, 2), 2) * 4 + lax.div(r_id, 4)
    mine = lax.div(l_id, 8) == group
    holder = jnp.sum(jnp.where(mine, spread[:16], 0.0), axis=0, keepdims=True)
    owner = jnp.sum(jnp.where(mine, spread[16:], 0.0), axis=0, keepdims=True)
    sub_f = sub.astype(F32)
    from_holder = hot(sub_f == holder)
    to_owner = hot(sub_f == owner)

    edges = jnp.concatenate([ed_ref[...], jnp.zeros((96, 128), F32)], axis=0).astype(BF16)
    stag_e[...] = mm(pick, edges, NT).reshape(NB, 1, 128)

    def lay(dst, src):
        for c in range(CT):
            tr_s[pl.ds(c, NB, stride=CT), :] = src[:, c * 128 : (c + 1) * 128]
        dst[...] = tr_s[...].reshape(NB, CT, 128).astype(BF16)

    def unlay(src):
        tr_s[...] = src[...].astype(F32).reshape(NB * CT, 128)

    for cc in range(NC):
        lay(stag.at[cc], mm(pick, st_ref[:, cc * CW : (cc + 1) * CW].astype(BF16)))

    pl.semaphore_wait(barrier, NB - 1 + NH - 1)
    to_all(stag_e, recv_e, ss_e.at[0], rs_e.at[0])

    def to_heads(src, dst, n):
        for i in range(1, NH):
            pltpu.make_async_remote_copy(
                src_ref=src(lax.rem(hd + i, NH)), dst_ref=dst.at[hd], send_sem=ss_h.at[n], recv_sem=rs_h.at[n],
                device_id=(me, lax.rem(hd + i, NH)), device_id_type=MESH,
            ).start()

    def heads_of(dst, n):
        return pltpu.make_async_remote_copy(
            src_ref=dst.at[pl.ds(0, NH - 1)], dst_ref=dst.at[pl.ds(0, NH - 1)],
            send_sem=ss_h.at[n], recv_sem=rs_h.at[n], device_id=(me, hd), device_id_type=MESH,
        )

    def part(g):
        return rq_ref.at[:, :, pl.ds(pl.multiple_of(g * WIDTH, WIDTH), WIDTH)]

    to_heads(part, r_recv, 0)

    xf = x_ref[...].astype(F32)
    xs[:, 8:24, :] = xf
    xs[:, 0:8, :] = jnp.zeros((REQ, 8, WIDTH), F32)
    prev = xs[:, 7:23, :]
    pb[...] = jnp.zeros(pb.shape, F32)

    def mix(cur, before, ratio):
        return (cur + (before - cur) * ratio).astype(BF16)

    delta_rows = (REQ * STEPS, WIDTH)
    md = mix(xf, prev, ratio_d[...].reshape(1, 1, WIDTH)).reshape(delta_rows)
    mr = mix(xf, prev, ratio_r[...].reshape(1, 1, WIDTH)).reshape(delta_rows)
    pb[0, :, 0:96] = mm(md, left_d[...], NT)
    pb[1, :, 0:96] = mm(mr, left_r[...], NT)
    to_heads(lambda g: pb, pr, 1)

    for cc in range(NC):
        to_all(stag.at[cc], recv.at[cc], ss.at[cc], rs.at[cc])
    recv_e[pl.ds(me, 1)] = stag_e[pl.ds(me, 1)]
    for cc in range(NC):
        recv[cc, pl.ds(me, 1)] = stag[cc, pl.ds(me, 1)]

    pr[pl.ds(hd, 1)] = pb[...].reshape(1, 2, NB, 128)
    r_recv[pl.ds(hd, 1)] = rq_ref[:, :, pl.ds(pl.multiple_of(hd * WIDTH, WIDTH), WIDTH)].reshape(
        1, REQ, 4, WIDTH
    )
    heads_of(r_recv, 0).wait_recv()
    for g in range(NH):
        r_r[:, 4 * g : 4 * g + 4, :] = r_recv[g].astype(F32)

    def put_rows(ref, val):
        for p in range(4):
            ref[p] = val[:, p * 128 : (p + 1) * 128]

    def get_rows(ref):
        return jnp.concatenate([ref[p] for p in range(4)], axis=1)

    def put_step(ref, t, val):
        for p in range(4):
            ref[p, pl.ds(t, REQ, stride=STEPS), :] = val[:, p * 128 : (p + 1) * 128]

    def second(summed_d, summed_r):
        hidden = jnp.tanh(summed_d[:, :96]).astype(BF16)
        zz = off_d[...] + mm(hidden, right_d[...])
        keep = jnp.exp(-DECAY_SCALE * jax.nn.sigmoid(zz))
        rate = jax.nn.sigmoid(off_r[...] + mm(summed_r[:, :96].astype(BF16), right_r[...]))
        return keep, rate

    kf = k_ref[...].astype(F32).reshape(delta_rows)
    put_rows(u_r, kf * erase[...])
    put_rows(v_r, v_ref[...].astype(F32).reshape(delta_rows))
    put_rows(r_s, r_r[...].reshape(delta_rows))

    heads_of(pr, 1).wait_recv()
    keep, rate = second(
        pr[0, 0] + pr[1, 0] + pr[2, 0] + pr[3, 0], pr[0, 1] + pr[1, 1] + pr[2, 1] + pr[3, 1]
    )
    put_rows(f_r, keep)
    put_rows(a_r, rate)
    put_rows(k_r, kf * (1.0 + (rate - 1.0) * written[...]))

    def turn(ref, tp):
        first = [ref[p, pl.ds(2 * tp, REQ, stride=STEPS), :] for p in range(4)]
        other = [ref[p, pl.ds(2 * tp + 1, REQ, stride=STEPS), :] for p in range(4)]
        rows = []
        for at in (0, 64):
            for p in range(4):
                rows.append(jnp.concatenate([first[p][:, at : at + 64], other[p][:, at : at + 64]], axis=1))
        return jnp.transpose(jnp.concatenate(rows + rows, axis=0))

    def turn_pair(tp, carry):
        def put_pair(dst, val):
            dst[pl.ds(2 * tp, 2)] = val.reshape(2, HW, 128)

        put_pair(f_t, turn(f_r, tp))
        put_pair(k_t, turn(k_r, tp))
        put_pair(r_t, turn(r_s, tp))
        u = turn(u_r, tp).reshape(2, HW, 128)
        u = u * lax.rsqrt(jnp.sum(u * u, axis=1, keepdims=True) + EPSILON)
        u_t[pl.ds(2 * tp, 2)] = u
        au_t[pl.ds(2 * tp, 2)] = turn(a_r, tp).reshape(2, HW, 128) * u
        return carry

    def turn_values(tq, carry):
        steps = [[v_r[p, pl.ds(4 * tq + i, REQ, stride=STEPS), :] for p in range(4)] for i in range(4)]
        rows = []
        for half in range(2):
            for odd in range(2):
                for p in range(4):
                    at = odd * 64 + half * 32
                    rows.append(jnp.concatenate([s[p][:, at : at + 32] for s in steps], axis=1))
        v_t[pl.ds(4 * tq, 4)] = jnp.transpose(jnp.concatenate(rows, axis=0)).reshape(4, ROWS, 128)
        return carry

    lax.fori_loop(0, 4, turn_values, 0)
    lax.fori_loop(1, 8, turn_pair, 0)

    all_of(stag_e, recv_e, ss_e.at[0], rs_e.at[0]).wait_recv()
    by_item = mm(from_holder, recv_e[...].reshape(NB, 128).astype(BF16), TN)
    edge_cols = []
    for p in range(4):
        parts = []
        for odd in range(2):
            for half in range(2):
                at = half * 64 + odd * 32 + p * 8
                parts.append(by_item[at : at + 8, 0:32])
        edge_cols.append(jnp.concatenate(parts, axis=1))
    edge = jnp.concatenate(edge_cols, axis=1)
    x0 = xs[:, 8, :]
    pb0[...] = jnp.zeros(pb0.shape, F32)
    pb0[0, :, 0:96] = mm(mix(x0, edge, ratio_d[...]), left_d[...], NT)
    pb0[1, :, 0:96] = mm(mix(x0, edge, ratio_r[...]), left_r[...], NT)
    to_heads(lambda g: pb0, pr0, 2)
    pr0[pl.ds(hd, 1)] = pb0[...].reshape(1, 2, REQ, 128)

    new_edge = jnp.where(count_col == 0, edge, 0.0)
    for t in range(STEPS):
        new_edge = new_edge + jnp.where(count_col == t + 1, xs[:, 8 + t, :], 0.0)
    items = []
    for half in range(2):
        for odd in range(2):
            for p in range(4):
                at = p * 128 + odd * 64 + half * 32
                items.append(new_edge[:, at : at + 32])
    items = jnp.concatenate(items, axis=0)
    items = jnp.concatenate([items, jnp.zeros((NB, 96), F32)], axis=1)
    back_es[...] = mm(to_owner, items.astype(BF16)).reshape(NB, 1, 128)
    to_all(back_es, back_er, ss_be.at[0], rs_be.at[0])
    back_er[pl.ds(me, 1)] = back_es[pl.ds(me, 1)]

    heads_of(pr0, 2).wait_recv()
    keep0, rate0 = second(
        pr0[0, 0] + pr0[1, 0] + pr0[2, 0] + pr0[3, 0], pr0[0, 1] + pr0[1, 1] + pr0[2, 1] + pr0[3, 1]
    )
    k0 = k_ref[...].astype(F32)[:, 0, :]
    put_step(f_r, 0, keep0)
    put_step(a_r, 0, rate0)
    put_step(k_r, 0, k0 * (1.0 + (rate0 - 1.0) * written[...]))
    turn_pair(0, 0)

    def advance_rows(row0, local0):
        start = [st_t[pl.ds(pl.multiple_of((local0 + i) * HW, HW), HW), :] for i in range(RB)]
        for i in range(RB):
            kept[pl.ds(pl.multiple_of((local0 + i) * HW, HW), HW), :] = start[i]

        def step(t, states):
            u, f, au, kk, r = u_t[t], f_t[t], au_t[t], k_t[t], r_t[t]
            taken = jnp.broadcast_to(count_row == t + 1, (HW, 128))
            out = []
            for i in range(RB):
                s = states[i]
                v = v_t[t, pl.ds(row0 + i, 1), :]
                proj = jnp.sum(s * u, axis=0, keepdims=True)
                s = s * f - proj * au + v * kk
                o_t[t, pl.ds(row0 + i, 1), :] = jnp.sum(s * r, axis=0, keepdims=True)
                where = pl.ds(pl.multiple_of((local0 + i) * HW, HW), HW)
                kept[where, :] = jnp.where(taken, s, kept[where, :])
                out.append(s)
            return tuple(out)

        lax.fori_loop(0, STEPS, step, tuple(start))

    for cc in range(NC):
        all_of(stag.at[cc], recv.at[cc], ss.at[cc], rs.at[cc]).wait_recv()
        unlay(recv.at[cc])
        for c in range(CT):
            block = tr_s[pl.ds(c, NB, stride=CT), :].astype(BF16)
            st_t[c * 128 : (c + 1) * 128, :] = mm(block, from_holder, TN)

        def rows(ib, carry):
            advance_rows(cc * CROWS + ib * RB, ib * RB)
            return carry

        lax.fori_loop(0, CROWS // RB, rows, 0)
        lay(back_s.at[cc], mm(to_owner, kept[...].astype(BF16), NT))
        to_all(back_s.at[cc], back_r.at[cc], ss_b.at[cc], rs_b.at[cc])
        back_r[cc, pl.ds(me, 1)] = back_s[cc, pl.ds(me, 1)]

    product = get_rows(r_s) * get_rows(k_r) * reward[...]
    high = product.astype(BF16)
    low = (product - high.astype(F32)).astype(BF16)
    b_row = lax.broadcasted_iota(I32, (WIDTH, WIDTH), 0)
    b_col = lax.broadcasted_iota(I32, (WIDTH, WIDTH), 1)
    same = hot(lax.div(b_row, HW) == lax.div(b_col, HW))
    bonus_s[...] = (mm(high, same) + mm(low, same)) * get_rows(v_r)

    def finish(tq, carry):
        o = o_t[pl.ds(4 * tq, 4)]
        total = jnp.sum(o, axis=1)
        mean = (total + pltpu.roll(total, 64, 1)) * (1.0 / HW)
        cen = o - mean.reshape(4, 1, 128)
        square = jnp.sum(cen * cen, axis=1)
        var = (square + pltpu.roll(square, 64, 1)) * (1.0 / HW)
        norm = cen * lax.rsqrt(var + NORM_EPSILON).reshape(4, 1, 128)
        flat = jnp.transpose(norm.reshape(128, 128))
        for i in range(4):
            pieces = []
            for p in range(4):
                for odd in range(2):
                    for half in range(2):
                        at = half * 64 + odd * 32 + p * 8
                        pieces.append(flat[at : at + 8, i * 32 : (i + 1) * 32])
            put_step(o_r, 4 * tq + i, jnp.concatenate(pieces, axis=1))
        return carry

    lax.fori_loop(0, 4, finish, 0)
    result = get_rows(o_r) * gain[...] + shift[...] + bonus_s[...]
    tb_ref[...] = result.astype(BF16).reshape(REQ, STEPS, WIDTH)

    all_of(back_es, back_er, ss_be.at[0], rs_be.at[0]).wait_recv()
    ne_ref[...] = mm(back_er[...].reshape(NB, 128).astype(BF16), put, TN)[0:32]
    for cc in range(NC):
        all_of(back_s.at[cc], back_r.at[cc], ss_b.at[cc], rs_b.at[cc]).wait_recv()
        unlay(back_r.at[cc])
        for c in range(CT):
            block = tr_s[pl.ds(c, NB, stride=CT), :].astype(BF16)
            at = cc * CW + c * 128
            ns_ref[:, at : at + 128] = mm(put, block, TN)

    all_of(stag_e, recv_e, ss_e.at[0], rs_e.at[0]).wait_send()
    all_of(back_es, back_er, ss_be.at[0], rs_be.at[0]).wait_send()
    for cc in range(NC):
        all_of(stag.at[cc], recv.at[cc], ss.at[cc], rs.at[cc]).wait_send()
        all_of(back_s.at[cc], back_r.at[cc], ss_b.at[cc], rs_b.at[cc]).wait_send()
    heads_of(r_recv, 0).wait_send()
    heads_of(pr, 1).wait_send()
    heads_of(pr0, 2).wait_send()


def local(
    layer_entry_vectors, guessed_lookup_vectors, guessed_content_vectors, gating_query,
    lane_memory_store, prior_step_store, fading_blend_ratio, learning_speed_blend,
    fading_left_factor, fading_right_factor, fading_offset,
    learning_speed_left, learning_speed_right, learning_speed_offset,
    erasing_lookup_factor, written_lookup_factor, present_reward_factors,
    lane_standard_factor, lane_standard_offset,
    caller_memory_directory, kept_target_place, caller_sequence, approved_guesses,
):
    def row(vector):
        return vector.reshape(1, WIDTH)

    vmem = pl.BlockSpec(memory_space=pltpu.VMEM)
    smem = pl.BlockSpec(memory_space=pltpu.SMEM)
    dma = pltpu.SemaphoreType.DMA
    rows = REQ * STEPS
    outs = pl.pallas_call(
        kernel,
        out_shape=(
            jax.ShapeDtypeStruct((REQ, STEPS, WIDTH), BF16),
            jax.ShapeDtypeStruct((NB, 2048), F32),
            jax.ShapeDtypeStruct((32, NB), F32),
        ),
        in_specs=[vmem] * 22 + [smem] * 2,
        out_specs=(vmem, vmem, vmem),
        scratch_shapes=[
            pltpu.VMEM((NC, NB, CT, 128), BF16),
            pltpu.VMEM((NC, NB, CT, 128), BF16),
            pltpu.VMEM((NB, 1, 128), F32),
            pltpu.VMEM((NB, 1, 128), F32),
            pltpu.VMEM((NC, NB, CT, 128), BF16),
            pltpu.VMEM((NC, NB, CT, 128), BF16),
            pltpu.VMEM((NB, 1, 128), F32),
            pltpu.VMEM((NB, 1, 128), F32),
            pltpu.VMEM((NH, REQ, 4, WIDTH), BF16),
            pltpu.VMEM((2, NB, 128), F32),
            pltpu.VMEM((NH, 2, NB, 128), F32),
            pltpu.VMEM((2, REQ, 128), F32),
            pltpu.VMEM((NH, 2, REQ, 128), F32),
            pltpu.VMEM((32, 1024), F32),
            pltpu.VMEM((NB * CT, 128), F32),
            pltpu.VMEM((REQ, 24, WIDTH), F32),
            pltpu.VMEM((CW, 128), F32),
            pltpu.VMEM((CW, 128), F32),
            pltpu.VMEM((4, rows, 128), F32),
            pltpu.VMEM((4, rows, 128), F32),
            pltpu.VMEM((4, rows, 128), F32),
            pltpu.VMEM((4, rows, 128), F32),
            pltpu.VMEM((REQ, STEPS, WIDTH), F32),
            pltpu.VMEM((4, rows, 128), F32),
            pltpu.VMEM((4, rows, 128), F32),
            pltpu.VMEM((4, rows, 128), F32),
            pltpu.VMEM((rows, WIDTH), F32),
            pltpu.VMEM((STEPS, HW, 128), F32),
            pltpu.VMEM((STEPS, HW, 128), F32),
            pltpu.VMEM((STEPS, HW, 128), F32),
            pltpu.VMEM((STEPS, HW, 128), F32),
            pltpu.VMEM((STEPS, HW, 128), F32),
            pltpu.VMEM((STEPS, ROWS, 128), F32),
            pltpu.VMEM((STEPS, ROWS, 128), F32),
            dma((NC,)), dma((NC,)), dma((1,)), dma((1,)),
            dma((NC,)), dma((NC,)), dma((1,)), dma((1,)), dma((3,)), dma((3,)),
        ],
        compiler_params=pltpu.CompilerParams(
            collective_id=0, has_side_effects=True, vmem_limit_bytes=56 << 20
        ),
        name="draft_check",
    )(
        layer_entry_vectors, guessed_lookup_vectors, guessed_content_vectors, gating_query,
        lane_memory_store.reshape(NB, 2048), jnp.transpose(prior_step_store[0]),
        row(fading_blend_ratio), row(learning_speed_blend), row(fading_offset), row(learning_speed_offset),
        row(erasing_lookup_factor), row(written_lookup_factor), row(present_reward_factors),
        row(lane_standard_factor), row(lane_standard_offset),
        jnp.transpose(fading_left_factor), fading_right_factor,
        jnp.transpose(learning_speed_left), learning_speed_right,
        jnp.transpose(caller_memory_directory, (1, 2, 0)), jnp.transpose(kept_target_place, (1, 2, 0)),
        caller_sequence.reshape(8, 128), caller_sequence, approved_guesses,
    )
    return (outs[0], outs[1][None], jnp.transpose(outs[2])[None])


def solution(mesh):
    return jax.shard_map(
        local,
        mesh=mesh,
        in_specs=(
            P("blk", None, "head"), P("blk", None, "head"), P("blk", None, "head"), P("blk", "head", None),
            P("head", "blk", None), P("head", "blk", None),
            P("head"), P("head"), P("head", None), P(None, "head"), P("head"),
            P("head", None), P(None, "head"), P("head"),
            P("head"), P("head"), P("head"), P("head"), P("head"),
            P(None, "head", None), P(None, "head", None), P(), P(),
        ),
        out_specs=(P("blk", None, "head"), P("head", "blk", None), P("head", "blk", None)),
        check_vma=False,
    )
```

time: 461 us -> 63.6 us (0.14)
  other arithmetic: 178 us -> 0 us
  local copies, waits for them, and re-layouts: 129 us -> 4.48 us
  starting transfers between devices: 84.2 us -> 0 us
  Pallas kernels: 0 us -> 58.3 us
  waiting for transfers between devices: 37.6 us -> 0 us
  blocking collectives: 13.9 us -> 0 us
  loops' own time: 11.1 us -> 0 us
    mul x33 -> x0, other arithmetic: 150 us -> none  [the longest x16 135 us: advance(): projected[..., None] * (rate_t * unit_t)[:, :, None, :]]
    all_to_all x7 -> x0, starting transfers between devices: 84.2 us -> none  [the longest x1 18.6 us: local(): lax.all_to_all(lane_memory_store[0][local_slots].reshape(blocks, per_peer...]
    pallas_call x0 -> x1, Pallas kernels: none -> 58.3 us  [local(): pl.pallas_call(kernel, out_shape=(jax.ShapeDtypeStruct((REQ, STEPS, WIDTH...]
    all_to_all x7 -> x0, waiting for transfers between devices: 37.6 us -> none  [the longest x1 21.5 us: local(): lax.all_to_all(send_states, 'blk', split_axis=0, concat_axis=0, tiled=True)]
    mul x51 -> x0, local copies, waits for them, and re-layouts: 37.5 us -> none  [the longest x16 12.5 us: advance(): output = jnp.sum(carry_state * recept_t[:, :, None, :], axis=-1)]
    gather x17 -> x0, local copies, waits for them, and re-layouts: 15.5 us -> none  [the longest x1 2.04 us: local(): got_states.reshape(slot_dev, slot_rows * head_width)[fetch_back]]
    unnamed x78 -> x5, local copies, waits for them, and re-layouts: 19.3 us -> 4.48 us
    psum x1 -> x0, blocking collectives: 13.9 us -> none  [local(): lax.psum(partial_terms.astype(jnp.bfloat16), 'head').astype(jnp.float32)]
  transfers between devices with their start and end apart: 7 -> 0, of which waited for: 4 -> 0; matrix products, arithmetic and copies ran while one was open for 61% -> 0% of each run, Pallas kernels for 0% -> 0%
where the time goes in v1:
time: 63.6 us; the launch traced here: 63.4 us
  Pallas kernels  58.3 us (92%)
  local copies, waits for them, and re-layouts  4.48 us (7%)
  between operations  0.65 us (1%)
    pallas_call x1, Pallas kernels, local(): pl.pallas_call(kernel, out_shape=(jax.ShapeDtypeStruct((REQ, STEPS, WIDTH...  58.3 us
    unnamed x5, local copies, waits for them, and re-layouts  4.48 us

profile of v1, /device:TPU:1, one launch (start us, length us, event | category | flops | bytes accessed | tf_op | source)
XLA Modules:
  0.0 63.4 jit_solution(18104121885611378258)
XLA Ops:
  0.6 58.3 %draft_check.1 = (bf16[8,16,512]{2,1,0:T(8,128)(2,1)}, f32[128,2048]{1,0:T(8,128)}, f32[32,128]{1,0:T(8,128)}) custom-call(bf16[8,16,512]{2,1,0:T(8,128)(2,1)} %x_ref.1, bf16[8,16,512]{2,1,0:T(8,128)(2,1)} %k_ref.1, bf16[8,16,512]{2,1,0:T(8,128)(2,1)} %v_ref.1, bf16[8,4,2048]{2,1,0:T(4,128)(2,1)} %rq_ref.1, f32[128,2048]{1,0:T(8,128)} %bitcast.22, ...), custom_call_target="tpu_custom_call" | custom-call | tf_op jit(solution)/shard_map/draft_check/pallas_call | solution.py:441
  58.9 1.6 %copy.29 = bf16[8,16,512]{2,1,0:T(8,128)(2,1)} copy(bf16[8,16,512]{2,1,0:T(8,128)(2,1)} %get-tuple-element.12) | data formatting | bytes 262144
  60.5 0.0 copy-start
  60.5 2.3 %copy.30 = f32[1,128,2048]{2,1,0:T(8,128)} copy(f32[1,128,2048]{2,1,0:T(8,128)} %bitcast.23) | data formatting | bytes 2097152
  62.8 0.0 copy-done
  62.8 0.6 copy.31
Async XLA Ops:
  60.5 2.3 %copy-start = (f32[32,128]{1,0:T(8,128)S(1)}, f32[32,128]{1,0:T(8,128)}, u32[]{:S(2)}) copy-start(f32[32,128]{1,0:T(8,128)} %get-tuple-element.8) | copy-start | bytes 49156

commit v2 on v1

--- a/solution.py
+++ b/solution.py
@@ -24,7 +24,8 @@
 HEADS = 8
 HW = 64
 ROWS = 32
-NC = 2
+NI = 24
+NC = 4
 CROWS = ROWS // NC
 CW = CROWS * HW
 CT = CW // 128
@@ -43,19 +44,25 @@
     return jnp.where(mask, 1.0, 0.0).astype(BF16)
 
 
-def kernel(
-    x_ref, k_ref, v_ref, rq_ref, st_ref, ed_ref,
-    ratio_d, ratio_r, off_d, off_r, erase, written, reward, gain, shift,
-    left_d, right_d, left_r, right_r,
-    dir_ref, tgt_ref, seqv_ref, seq_sm, app_sm,
-    tb_ref, ns_ref, ne_ref,
-    stag, recv, stag_e, recv_e, back_s, back_r, back_es, back_er,
-    r_recv, pb, pr, pb0, pr0,
-    hi_s, tr_s, xs, kept, st_t,
-    f_r, u_r, a_r, k_r, r_r, r_s, v_r, o_r, bonus_s,
-    f_t, u_t, au_t, k_t, r_t, v_t, o_t,
-    ss, rs, ss_e, rs_e, ss_b, rs_b, ss_be, rs_be, ss_h, rs_h,
-):
+def kernel(*refs):
+    hbm, (tb_ref, back_r, back_er, put_ref) = refs[:NI], refs[NI : NI + 4]
+    held, ss_i = refs[NI + 4 : 2 * NI + 4], refs[2 * NI + 4]
+    loads = [pltpu.make_async_copy(hbm[i], held[i], ss_i.at[i]) for i in range(NI)]
+    for i in (21, 19, 20, 22, 23, 4, 5, 3, 0, 1, 2) + tuple(range(6, 19)):
+        loads[i].start()
+    (
+        x_ref, k_ref, v_ref, rq_ref, st_ref, ed_ref,
+        ratio_d, ratio_r, off_d, off_r, erase, written, reward, gain, shift,
+        left_d, right_d, left_r, right_r, dir_ref, tgt_ref, seqv_ref, seq_sm, app_sm,
+    ) = held
+    (
+        stag, mid, recv, stag_e, mid_e, recv_e, back_s, back_m, back_es, back_em,
+        r_recv, pb, pr, pb0, pr0,
+        hi_s, tr_s, xs, kept, st_t,
+        f_r, u_r, a_r, k_r, r_r, r_s, v_r, o_r, bonus_s,
+        f_t, u_t, au_t, k_t, r_t, v_t, o_t,
+        ss_e, rs_e, ss_h, rs_h,
+    ) = refs[2 * NI + 5 :]
     me = lax.axis_index("blk")
     hd = lax.axis_index("head")
     z = lax.div(me, 16)
@@ -68,42 +75,54 @@
     inner = [(b, c) for b in far for c in (1, 0)]
 
     barrier = pltpu.get_barrier_semaphore()
-    for a in far:
-        for b, c in inner:
-            if a or b or c:
-                pl.semaphore_signal(
-                    barrier, inc=1, device_id=(z_off[a] + y_off[b] + c_off[c], hd), device_id_type=MESH
-                )
+    for a in far[:-1]:
+        pl.semaphore_signal(
+            barrier, inc=1, device_id=(z_off[a] + lax.rem(me, 16), hd), device_id_type=MESH
+        )
+    for b, c in inner[:-1]:
+        pl.semaphore_signal(
+            barrier, inc=1, device_id=(z_off[0] + y_off[b] + c_off[c], hd), device_id_type=MESH
+        )
     for i in range(1, NH):
         pl.semaphore_signal(barrier, inc=1, device_id=(me, lax.rem(hd + i, NH)), device_id_type=MESH)
-
-    def to_all(src, dst, send_sem, recv_sem):
-        def start(d):
-            pltpu.make_async_remote_copy(
-                src_ref=src.at[d], dst_ref=dst.at[me], send_sem=send_sem, recv_sem=recv_sem,
-                device_id=(d, hd), device_id_type=MESH,
-            ).start()
-
-        def ring(a, carry):
-            dz = 4 + lax.div(a + 1, 2) * (1 - 2 * lax.rem(a, 2))
-            base = lax.rem(z + dz, 8) * 16
-            for b, c in inner:
-                start(base + y_off[b] + c_off[c])
-            return carry
-
-        lax.fori_loop(0, 7, ring, 0)
-        for b, c in inner[:-1]:
-            start(z_off[0] + y_off[b] + c_off[c])
-
-    def all_of(src, dst, send_sem, recv_sem):
-        return pltpu.make_async_remote_copy(
-            src_ref=src.at[pl.ds(0, NB - 1)], dst_ref=dst.at[pl.ds(0, NB - 1)],
-            send_sem=send_sem, recv_sem=recv_sem, device_id=(me, hd), device_id_type=MESH,
-        )
 
     lane = lax.broadcasted_iota(I32, (NB, 128), 1)
     sub = lax.broadcasted_iota(I32, (NB, 128), 0)
     lane_f = lane.astype(F32)
+
+    w = lax.rem(me, 16)
+
+    def hop_z(src, dst, n):
+        for a in far[:-1]:
+            pltpu.make_async_remote_copy(
+                src_ref=src.at[lax.rem(z + a, 8)], dst_ref=dst.at[z], send_sem=ss_e.at[n], recv_sem=rs_e.at[n],
+                device_id=(z_off[a] + w, hd), device_id_type=MESH,
+            ).start()
+        dst[pl.ds(z, 1)] = src[pl.ds(z, 1)]
+
+    def hop_w(src, dst, n):
+        for b, c in inner[:-1]:
+            to = y_off[b] + c_off[c]
+            pltpu.make_async_remote_copy(
+                src_ref=src.at[:, to], dst_ref=dst.at[:, w], send_sem=ss_e.at[n], recv_sem=rs_e.at[n],
+                device_id=(z_off[0] + to, hd), device_id_type=MESH,
+            ).start()
+        dst[:, pl.ds(w, 1)] = src[:, pl.ds(w, 1)]
+
+    def all_z(src, dst, n):
+        return pltpu.make_async_remote_copy(
+            src_ref=src.at[pl.ds(0, 7)], dst_ref=dst.at[pl.ds(0, 7)],
+            send_sem=ss_e.at[n], recv_sem=rs_e.at[n], device_id=(me, hd), device_id_type=MESH,
+        )
+
+    def all_w(src, dst, n):
+        return pltpu.make_async_remote_copy(
+            src_ref=src.at[:, pl.ds(0, 15)], dst_ref=dst.at[:, pl.ds(0, 15)],
+            send_sem=ss_e.at[n], recv_sem=rs_e.at[n], device_id=(me, hd), device_id_type=MESH,
+        )
+
+    for i in (21, 19, 20, 22, 23):
+        loads[i].wait()
 
     fetch_q = jnp.zeros((2, 1024), I32)
     place_q = jnp.zeros((2, 1024), I32)
@@ -130,7 +149,7 @@
     place = jnp.floor(both * (1.0 / 128.0))
     fetch = both - 128.0 * place
     pick = hot(fetch == lane_f)
-    put = hot(place == lane_f)
+    put_ref[...] = hot(place == lane_f)
 
     row8 = lax.broadcasted_iota(I32, (REQ, 1024), 0)
     lane1024 = lax.broadcasted_iota(I32, (REQ, 1024), 1)
@@ -158,23 +177,48 @@
     from_holder = hot(sub_f == holder)
     to_owner = hot(sub_f == owner)
 
+    loads[4].wait()
+    loads[5].wait()
     edges = jnp.concatenate([ed_ref[...], jnp.zeros((96, 128), F32)], axis=0).astype(BF16)
-    stag_e[...] = mm(pick, edges, NT).reshape(NB, 1, 128)
-
-    def lay(dst, src):
-        for c in range(CT):
-            tr_s[pl.ds(c, NB, stride=CT), :] = src[:, c * 128 : (c + 1) * 128]
-        dst[...] = tr_s[...].reshape(NB, CT, 128).astype(BF16)
-
-    def unlay(src):
-        tr_s[...] = src[...].astype(F32).reshape(NB * CT, 128)
+    stag_e[...] = mm(pick, edges, NT).reshape(8, 16, 1, 128)
+
+    def lay(dst, src, ct):
+        for c in range(ct):
+            tr_s[pl.ds(c, NB, stride=ct), :] = src[:, c * 128 : (c + 1) * 128]
+        dst[...] = tr_s[pl.ds(0, NB * ct), :].reshape(dst.shape).astype(BF16)
 
     for cc in range(NC):
-        lay(stag.at[cc], mm(pick, st_ref[:, cc * CW : (cc + 1) * CW].astype(BF16)))
-
-    pl.semaphore_wait(barrier, NB - 1 + NH - 1)
-    to_all(stag_e, recv_e, ss_e.at[0], rs_e.at[0])
-
+        lay(stag.at[cc], mm(pick, st_ref[:, cc * CW : (cc + 1) * CW].astype(BF16)), CT)
+
+    def first_hop(src, dst, cc, n):
+        (hop_w if cc % 2 else hop_z)(src.at[cc], dst.at[cc], n + 2 * cc)
+
+    def first_all(src, dst, cc, n):
+        return (all_w if cc % 2 else all_z)(src.at[cc], dst.at[cc], n + 2 * cc)
+
+    def second_hop(src, dst, cc, n):
+        (hop_z if cc % 2 else hop_w)(src.at[cc], dst.at[cc], n + 1 + 2 * cc)
+
+    def second_all(src, dst, cc, n):
+        return (all_z if cc % 2 else all_w)(src.at[cc], dst.at[cc], n + 1 + 2 * cc)
+
+    fetch_n, back_n = 4, 4 + 2 * NC
+
+    for i in (3, 0, 1, 2) + tuple(range(6, 19)):
+        loads[i].wait()
+    xf = x_ref[...].astype(F32)
+    xs[:, 8:24, :] = xf
+    xs[:, 0:8, :] = jnp.zeros((REQ, 8, WIDTH), F32)
+    prev = xs[:, 7:23, :]
+
+    def mix(cur, before, ratio):
+        return (cur + (before - cur) * ratio).astype(BF16)
+
+    delta_rows = (REQ * STEPS, WIDTH)
+    md = mix(xf, prev, ratio_d[...].reshape(1, 1, WIDTH)).reshape(delta_rows)
+    mr = mix(xf, prev, ratio_r[...].reshape(1, 1, WIDTH)).reshape(delta_rows)
+    pb[0] = mm(left_d[...], md, NT).astype(BF16)
+    pb[1] = mm(left_r[...], mr, NT).astype(BF16)
     def to_heads(src, dst, n):
         for i in range(1, NH):
             pltpu.make_async_remote_copy(
@@ -191,31 +235,14 @@
     def part(g):
         return rq_ref.at[:, :, pl.ds(pl.multiple_of(g * WIDTH, WIDTH), WIDTH)]
 
+    pl.semaphore_wait(barrier, 7 + 15 + NH - 1)
+    hop_z(stag_e, mid_e, 0)
     to_heads(part, r_recv, 0)
-
-    xf = x_ref[...].astype(F32)
-    xs[:, 8:24, :] = xf
-    xs[:, 0:8, :] = jnp.zeros((REQ, 8, WIDTH), F32)
-    prev = xs[:, 7:23, :]
-    pb[...] = jnp.zeros(pb.shape, F32)
-
-    def mix(cur, before, ratio):
-        return (cur + (before - cur) * ratio).astype(BF16)
-
-    delta_rows = (REQ * STEPS, WIDTH)
-    md = mix(xf, prev, ratio_d[...].reshape(1, 1, WIDTH)).reshape(delta_rows)
-    mr = mix(xf, prev, ratio_r[...].reshape(1, 1, WIDTH)).reshape(delta_rows)
-    pb[0, :, 0:96] = mm(md, left_d[...], NT)
-    pb[1, :, 0:96] = mm(mr, left_r[...], NT)
     to_heads(lambda g: pb, pr, 1)
-
-    for cc in range(NC):
-        to_all(stag.at[cc], recv.at[cc], ss.at[cc], rs.at[cc])
-    recv_e[pl.ds(me, 1)] = stag_e[pl.ds(me, 1)]
-    for cc in range(NC):
-        recv[cc, pl.ds(me, 1)] = stag[cc, pl.ds(me, 1)]
-
-    pr[pl.ds(hd, 1)] = pb[...].reshape(1, 2, NB, 128)
+    first_hop(stag, mid, 0, fetch_n)
+    first_hop(stag, mid, 1, fetch_n)
+
+    pr[pl.ds(hd, 1)] = pb[...].reshape(1, 2, 96, 128)
     r_recv[pl.ds(hd, 1)] = rq_ref[:, :, pl.ds(pl.multiple_of(hd * WIDTH, WIDTH), WIDTH)].reshape(
         1, REQ, 4, WIDTH
     )
@@ -234,11 +261,11 @@
         for p in range(4):
             ref[p, pl.ds(t, REQ, stride=STEPS), :] = val[:, p * 128 : (p + 1) * 128]
 
-    def second(summed_d, summed_r):
-        hidden = jnp.tanh(summed_d[:, :96]).astype(BF16)
-        zz = off_d[...] + mm(hidden, right_d[...])
+    def second(summed_d, summed_r, dims):
+        hidden = jnp.tanh(summed_d).astype(BF16)
+        zz = off_d[...] + mm(hidden, right_d[...], dims)
         keep = jnp.exp(-DECAY_SCALE * jax.nn.sigmoid(zz))
-        rate = jax.nn.sigmoid(off_r[...] + mm(summed_r[:, :96].astype(BF16), right_r[...]))
+        rate = jax.nn.sigmoid(off_r[...] + mm(summed_r.astype(BF16), right_r[...], dims))
         return keep, rate
 
     kf = k_ref[...].astype(F32).reshape(delta_rows)
@@ -247,9 +274,8 @@
     put_rows(r_s, r_r[...].reshape(delta_rows))
 
     heads_of(pr, 1).wait_recv()
-    keep, rate = second(
-        pr[0, 0] + pr[1, 0] + pr[2, 0] + pr[3, 0], pr[0, 1] + pr[1, 1] + pr[2, 1] + pr[3, 1]
-    )
+    sums = pr[0].astype(F32) + pr[1].astype(F32) + pr[2].astype(F32) + pr[3].astype(F32)
+    keep, rate = second(sums[0], sums[1], TN)
     put_rows(f_r, keep)
     put_rows(a_r, rate)
     put_rows(k_r, kf * (1.0 + (rate - 1.0) * written[...]))
@@ -288,9 +314,21 @@
         return carry
 
     lax.fori_loop(0, 4, turn_values, 0)
+
+    all_z(stag_e, mid_e, 0).wait_recv()
+    hop_w(mid_e, recv_e, 1)
+    first_hop(stag, mid, 2, fetch_n)
+    first_hop(stag, mid, 3, fetch_n)
     lax.fori_loop(1, 8, turn_pair, 0)
 
-    all_of(stag_e, recv_e, ss_e.at[0], rs_e.at[0]).wait_recv()
+    def pass_on(cc):
+        first_all(stag, mid, cc, fetch_n).wait_recv()
+        second_hop(mid, recv, cc, fetch_n)
+
+    pass_on(0)
+    pass_on(1)
+
+    all_w(mid_e, recv_e, 1).wait_recv()
     by_item = mm(from_holder, recv_e[...].reshape(NB, 128).astype(BF16), TN)
     edge_cols = []
     for p in range(4):
@@ -308,6 +346,7 @@
     to_heads(lambda g: pb0, pr0, 2)
     pr0[pl.ds(hd, 1)] = pb0[...].reshape(1, 2, REQ, 128)
 
+
     new_edge = jnp.where(count_col == 0, edge, 0.0)
     for t in range(STEPS):
         new_edge = new_edge + jnp.where(count_col == t + 1, xs[:, 8 + t, :], 0.0)
@@ -319,14 +358,14 @@
                 items.append(new_edge[:, at : at + 32])
     items = jnp.concatenate(items, axis=0)
     items = jnp.concatenate([items, jnp.zeros((NB, 96), F32)], axis=1)
-    back_es[...] = mm(to_owner, items.astype(BF16)).reshape(NB, 1, 128)
-    to_all(back_es, back_er, ss_be.at[0], rs_be.at[0])
-    back_er[pl.ds(me, 1)] = back_es[pl.ds(me, 1)]
-
+    back_es[...] = mm(to_owner, items.astype(BF16)).reshape(8, 16, 1, 128)
+    hop_z(back_es, back_em, 2)
+
+    pass_on(2)
+    pass_on(3)
     heads_of(pr0, 2).wait_recv()
-    keep0, rate0 = second(
-        pr0[0, 0] + pr0[1, 0] + pr0[2, 0] + pr0[3, 0], pr0[0, 1] + pr0[1, 1] + pr0[2, 1] + pr0[3, 1]
-    )
+    sums0 = (pr0[0] + pr0[1] + pr0[2] + pr0[3])[:, :, :96]
+    keep0, rate0 = second(sums0[0], sums0[1], NN)
     k0 = k_ref[...].astype(F32)[:, 0, :]
     put_step(f_r, 0, keep0)
     put_step(a_r, 0, rate0)
@@ -355,21 +394,29 @@
 
         lax.fori_loop(0, STEPS, step, tuple(start))
 
+    def return_on(cc):
+        first_all(back_s, back_m, cc, back_n).wait_recv()
+        second_hop(back_m, back_r, cc, back_n)
+
     for cc in range(NC):
-        all_of(stag.at[cc], recv.at[cc], ss.at[cc], rs.at[cc]).wait_recv()
-        unlay(recv.at[cc])
+        second_all(mid, recv, cc, fetch_n).wait_recv()
+        tr_s[...] = recv[cc].astype(F32).reshape(NB * CT, 128)
         for c in range(CT):
             block = tr_s[pl.ds(c, NB, stride=CT), :].astype(BF16)
             st_t[c * 128 : (c + 1) * 128, :] = mm(block, from_holder, TN)
 
-        def rows(ib, carry):
+        def rows(ib, carry, cc=cc):
             advance_rows(cc * CROWS + ib * RB, ib * RB)
             return carry
 
         lax.fori_loop(0, CROWS // RB, rows, 0)
-        lay(back_s.at[cc], mm(to_owner, kept[...].astype(BF16), NT))
-        to_all(back_s.at[cc], back_r.at[cc], ss_b.at[cc], rs_b.at[cc])
-        back_r[cc, pl.ds(me, 1)] = back_s[cc, pl.ds(me, 1)]
+        lay(back_s.at[cc], mm(to_owner, kept[...].astype(BF16), NT), CT)
+        first_hop(back_s, back_m, cc, back_n)
+        if cc == 0:
+            all_z(back_es, back_em, 2).wait_recv()
+            hop_w(back_em, back_er, 3)
+        if cc >= 2:
+            return_on(cc - 2)
 
     product = get_rows(r_s) * get_rows(k_r) * reward[...]
     high = product.astype(BF16)
@@ -378,6 +425,8 @@
     b_col = lax.broadcasted_iota(I32, (WIDTH, WIDTH), 1)
     same = hot(lax.div(b_row, HW) == lax.div(b_col, HW))
     bonus_s[...] = (mm(high, same) + mm(low, same)) * get_rows(v_r)
+
+    return_on(NC - 2)
 
     def finish(tq, carry):
         o = o_t[pl.ds(4 * tq, 4)]
@@ -399,27 +448,38 @@
         return carry
 
     lax.fori_loop(0, 4, finish, 0)
+    return_on(NC - 1)
     result = get_rows(o_r) * gain[...] + shift[...] + bonus_s[...]
     tb_ref[...] = result.astype(BF16).reshape(REQ, STEPS, WIDTH)
 
-    all_of(back_es, back_er, ss_be.at[0], rs_be.at[0]).wait_recv()
+    all_w(back_em, back_er, 3).wait_recv()
+    for cc in range(NC):
+        second_all(back_m, back_r, cc, back_n).wait_recv()
+    all_z(stag_e, mid_e, 0).wait_send()
+    all_w(mid_e, recv_e, 1).wait_send()
+    all_z(back_es, back_em, 2).wait_send()
+    all_w(back_em, back_er, 3).wait_send()
+    for cc in range(NC):
+        first_all(stag, mid, cc, fetch_n).wait_send()
+        second_all(mid, recv, cc, fetch_n).wait_send()
+        first_all(back_s, back_m, cc, back_n).wait_send()
+        second_all(back_m, back_r, cc, back_n).wait_send()
+    heads_of(r_recv, 0).wait_send()
+    heads_of(pr, 1).wait_send()
+    heads_of(pr0, 2).wait_send()
+
+
+def settle(tb_ref, back_r, back_er, put_ref, out_ref, ns_ref, ne_ref, tr_s):
+    out_ref[...] = tb_ref[...]
+    put = put_ref[...]
     ne_ref[...] = mm(back_er[...].reshape(NB, 128).astype(BF16), put, TN)[0:32]
+    put_t = jnp.transpose(put.astype(F32)).astype(BF16)
     for cc in range(NC):
-        all_of(back_s.at[cc], back_r.at[cc], ss_b.at[cc], rs_b.at[cc]).wait_recv()
-        unlay(back_r.at[cc])
+        tr_s[...] = back_r[cc].astype(F32).reshape(NB * CT, 128)
         for c in range(CT):
             block = tr_s[pl.ds(c, NB, stride=CT), :].astype(BF16)
             at = cc * CW + c * 128
-            ns_ref[:, at : at + 128] = mm(put, block, TN)
-
-    all_of(stag_e, recv_e, ss_e.at[0], rs_e.at[0]).wait_send()
-    all_of(back_es, back_er, ss_be.at[0], rs_be.at[0]).wait_send()
-    for cc in range(NC):
-        all_of(stag.at[cc], recv.at[cc], ss.at[cc], rs.at[cc]).wait_send()
-        all_of(back_s.at[cc], back_r.at[cc], ss_b.at[cc], rs_b.at[cc]).wait_send()
-    heads_of(r_recv, 0).wait_send()
-    heads_of(pr, 1).wait_send()
-    heads_of(pr0, 2).wait_send()
+            ns_ref[:, at : at + 128] = mm(put_t, block)
 
 
 def local(
@@ -435,30 +495,47 @@
         return vector.reshape(1, WIDTH)
 
     vmem = pl.BlockSpec(memory_space=pltpu.VMEM)
-    smem = pl.BlockSpec(memory_space=pltpu.SMEM)
     dma = pltpu.SemaphoreType.DMA
     rows = REQ * STEPS
+    arrays = (
+        layer_entry_vectors, guessed_lookup_vectors, guessed_content_vectors, gating_query,
+        lane_memory_store.reshape(NB, 2048), jnp.transpose(prior_step_store[0]),
+        row(fading_blend_ratio), row(learning_speed_blend), row(fading_offset), row(learning_speed_offset),
+        row(erasing_lookup_factor), row(written_lookup_factor), row(present_reward_factors),
+        row(lane_standard_factor), row(lane_standard_offset),
+        jnp.transpose(fading_left_factor), fading_right_factor,
+        jnp.transpose(learning_speed_left), learning_speed_right,
+        jnp.transpose(caller_memory_directory, (1, 2, 0)), jnp.transpose(kept_target_place, (1, 2, 0)),
+        caller_sequence.reshape(8, 128), caller_sequence, approved_guesses,
+    )
+    hbm = pl.BlockSpec(memory_space=pltpu.HBM)
     outs = pl.pallas_call(
         kernel,
         out_shape=(
             jax.ShapeDtypeStruct((REQ, STEPS, WIDTH), BF16),
-            jax.ShapeDtypeStruct((NB, 2048), F32),
-            jax.ShapeDtypeStruct((32, NB), F32),
+            jax.ShapeDtypeStruct((NC, 8, 16, CT, 128), BF16),
+            jax.ShapeDtypeStruct((8, 16, 1, 128), F32),
+            jax.ShapeDtypeStruct((NB, 128), BF16),
         ),
-        in_specs=[vmem] * 22 + [smem] * 2,
-        out_specs=(vmem, vmem, vmem),
-        scratch_shapes=[
-            pltpu.VMEM((NC, NB, CT, 128), BF16),
-            pltpu.VMEM((NC, NB, CT, 128), BF16),
-            pltpu.VMEM((NB, 1, 128), F32),
-            pltpu.VMEM((NB, 1, 128), F32),
-            pltpu.VMEM((NC, NB, CT, 128), BF16),
-            pltpu.VMEM((NC, NB, CT, 128), BF16),
-            pltpu.VMEM((NB, 1, 128), F32),
-            pltpu.VMEM((NB, 1, 128), F32),
+        in_specs=[hbm] * NI,
+        out_specs=(vmem,) * 4,
+        scratch_shapes=[pltpu.VMEM(a.shape, a.dtype) for a in arrays[:-2]]
+        + [pltpu.SMEM(a.shape, a.dtype) for a in arrays[-2:]]
+        + [
+            dma((NI,)),
+            pltpu.VMEM((NC, 8, 16, CT, 128), BF16),
+            pltpu.VMEM((NC, 8, 16, CT, 128), BF16),
+            pltpu.VMEM((NC, 8, 16, CT, 128), BF16),
+            pltpu.VMEM((8, 16, 1, 128), F32),
+            pltpu.VMEM((8, 16, 1, 128), F32),
+            pltpu.VMEM((8, 16, 1, 128), F32),
+            pltpu.VMEM((NC, 8, 16, CT, 128), BF16),
+            pltpu.VMEM((NC, 8, 16, CT, 128), BF16),
+            pltpu.VMEM((8, 16, 1, 128), F32),
+            pltpu.VMEM((8, 16, 1, 128), F32),
             pltpu.VMEM((NH, REQ, 4, WIDTH), BF16),
-            pltpu.VMEM((2, NB, 128), F32),
-            pltpu.VMEM((NH, 2, NB, 128), F32),
+            pltpu.VMEM((2, 96, 128), BF16),
+            pltpu.VMEM((NH, 2, 96, 128), BF16),
             pltpu.VMEM((2, REQ, 128), F32),
             pltpu.VMEM((NH, 2, REQ, 128), F32),
             pltpu.VMEM((32, 1024), F32),
@@ -482,25 +559,29 @@
             pltpu.VMEM((STEPS, HW, 128), F32),
             pltpu.VMEM((STEPS, ROWS, 128), F32),
             pltpu.VMEM((STEPS, ROWS, 128), F32),
-            dma((NC,)), dma((NC,)), dma((1,)), dma((1,)),
-            dma((NC,)), dma((NC,)), dma((1,)), dma((1,)), dma((3,)), dma((3,)),
+            dma((4 + 4 * NC,)), dma((4 + 4 * NC,)), dma((3,)), dma((3,)),
         ],
         compiler_params=pltpu.CompilerParams(
-            collective_id=0, has_side_effects=True, vmem_limit_bytes=56 << 20
+            collective_id=0, has_side_effects=True, vmem_limit_bytes=24 << 20
         ),
         name="draft_check",
     )(
-        layer_entry_vectors, guessed_lookup_vectors, guessed_content_vectors, gating_query,
-        lane_memory_store.reshape(NB, 2048), jnp.transpose(prior_step_store[0]),
-        row(fading_blend_ratio), row(learning_speed_blend), row(fading_offset), row(learning_speed_offset),
-        row(erasing_lookup_factor), row(written_lookup_factor), row(present_reward_factors),
-        row(lane_standard_factor), row(lane_standard_offset),
-        jnp.transpose(fading_left_factor), fading_right_factor,
-        jnp.transpose(learning_speed_left), learning_speed_right,
-        jnp.transpose(caller_memory_directory, (1, 2, 0)), jnp.transpose(kept_target_place, (1, 2, 0)),
-        caller_sequence.reshape(8, 128), caller_sequence, approved_guesses,
+        *[pltpu.with_memory_space_constraint(a, pltpu.HBM) for a in arrays]
     )
-    return (outs[0], outs[1][None], jnp.transpose(outs[2])[None])
+    result, states, edges = pl.pallas_call(
+        settle,
+        out_shape=(
+            jax.ShapeDtypeStruct((REQ, STEPS, WIDTH), BF16),
+            jax.ShapeDtypeStruct((NB, 2048), F32),
+            jax.ShapeDtypeStruct((32, NB), F32),
+        ),
+        in_specs=[vmem] * 4,
+        out_specs=(vmem,) * 3,
+        scratch_shapes=[pltpu.VMEM((NB * CT, 128), F32)],
+        compiler_params=pltpu.CompilerParams(vmem_limit_bytes=12 << 20),
+        name="settle",
+    )(*outs)
+    return (result, states[None], jnp.transpose(edges)[None])
 
 
 def solution(mesh):

time: 63.6 us -> 58.5 us (0.920)
  local copies, waits for them, and re-layouts: 4.48 us -> 0 us
    unnamed x5 -> x0, local copies, waits for them, and re-layouts: 4.48 us -> none
    pallas_call x1, Pallas kernels: 58.3 us -> 56.3 us  [local(): pl.pallas_call(kernel, out_shape=(jax.ShapeDtypeStruct((REQ, STEPS, WIDTH...]
    pallas_call x0 -> x1, Pallas kernels: none -> 1.43 us  [local(): pl.pallas_call(settle, out_shape=(jax.ShapeDtypeStruct((REQ, STEPS, WIDTH...]
where the time goes in v2:
time: 58.5 us; the launch traced here: 58.4 us
  Pallas kernels  57.7 us (99%)
  between operations  0.65 us (1%)
    pallas_call x1, Pallas kernels, local(): pl.pallas_call(kernel, out_shape=(jax.ShapeDtypeStruct((REQ, STEPS, WIDTH...  56.3 us
    pallas_call x1, Pallas kernels, local(): pl.pallas_call(settle, out_shape=(jax.ShapeDtypeStruct((REQ, STEPS, WIDTH...  1.43 us

profile of v2, /device:TPU:1, one launch (start us, length us, event | category | flops | bytes accessed | tf_op | source)
XLA Modules:
  0.0 58.4 jit_solution(5552603766226125)
XLA Ops:
  0.6 56.3 %draft_check.1 = (bf16[8,16,512]{2,1,0:T(8,128)(2,1)S(1)}, bf16[4,8,16,4,128]{4,3,2,1,0:T(4,128)(2,1)S(1)}, f32[8,16,1,128]{3,2,1,0:T(1,128)S(1)}, bf16[128,128]{1,0:T(8,128)(2,1)S(1)}) custom-call(bf16[8,16,512]{2,1,0:T(8,128)(2,1)} %refs_0_.1, bf16[8,16,512]{2,1,0:T(8,128)(2,1)} %refs_1_.1, bf16[8,16,512]{2,1,0:T(8,128)(2,1)} %refs_2_.1, ...), custom_call_target="tpu_custom_call" | custom-call | tf_op jit(solution)/shard_map/draft_check/pallas_call | solution.py:512
  57.0 1.4 %settle.1 = (bf16[8,16,512]{2,1,0:T(8,128)(2,1)}, f32[128,2048]{1,0:T(8,128)}, f32[32,128]{1,0:T(8,128)}) custom-call(bf16[8,16,512]{2,1,0:T(8,128)(2,1)S(1)} %get-tuple-element.10.tb_ref, bf16[4,8,16,4,128]{4,3,2,1,0:T(4,128)(2,1)S(1)} %get-tuple-element.11.back_r, f32[8,16,1,128]{3,2,1,0:T(1,128)S(1)} %get-tuple-element.12.back_er, ...), custom_call_target="tpu_custom_call" | custom-call | tf_op jit(solution)/shard_map/settle/pallas_call | solution.py:571

commit v3 on v2

--- a/solution.py
+++ b/solution.py
@@ -29,6 +29,7 @@
 CROWS = ROWS // NC
 CW = CROWS * HW
 CT = CW // 128
+CS = CT // 2
 RB = 4
 
 NT = (((1,), (1,)), ((), ()))
@@ -151,6 +152,99 @@
     pick = hot(fetch == lane_f)
     put_ref[...] = hot(place == lane_f)
 
+    loads[5].wait()
+    edges = jnp.concatenate([ed_ref[...], jnp.zeros((96, 128), F32)], axis=0).astype(BF16)
+    stag_e[...] = mm(pick, edges, NT).reshape(8, 16, 1, 128)
+
+    def lay(dst, src, ct):
+        for c in range(ct):
+            tr_s[pl.ds(c, NB, stride=ct), :] = src[:, c * 128 : (c + 1) * 128]
+        dst[...] = tr_s[pl.ds(0, NB * ct), :].reshape(dst.shape).astype(BF16)
+
+    def lay_piece(dst, src):
+        for half in range(2):
+            lay(dst.at[half], src[:, half * CS * 128 : (half + 1) * CS * 128], CS)
+
+    def gather(cc):
+        lay_piece(stag.at[cc], mm(pick, st_ref[:, cc * CW : (cc + 1) * CW].astype(BF16)))
+        first_hop(stag, mid, cc, fetch_n)
+
+    def first_hop(src, dst, cc, n):
+        hop_z(src.at[cc, 0], dst.at[cc, 0], n + 4 * cc)
+        hop_w(src.at[cc, 1], dst.at[cc, 1], n + 4 * cc + 1)
+
+    def first_all(src, dst, cc, n):
+        return (
+            all_z(src.at[cc, 0], dst.at[cc, 0], n + 4 * cc),
+            all_w(src.at[cc, 1], dst.at[cc, 1], n + 4 * cc + 1),
+        )
+
+    def second_hop(src, between, dst, cc, n):
+        first_z, first_w = first_all(src, between, cc, n)
+        first_z.wait_recv()
+        hop_w(between.at[cc, 0], dst.at[cc, 0], n + 4 * cc + 2)
+        first_w.wait_recv()
+        hop_z(between.at[cc, 1], dst.at[cc, 1], n + 4 * cc + 3)
+
+    def second_all(src, dst, cc, n):
+        return (
+            all_w(src.at[cc, 0], dst.at[cc, 0], n + 4 * cc + 2),
+            all_z(src.at[cc, 1], dst.at[cc, 1], n + 4 * cc + 3),
+        )
+
+    def received(copies):
+        for copy in copies:
+            copy.wait_recv()
+
+    def sent(copies):
+        for copy in copies:
+            copy.wait_send()
+
+    fetch_n, back_n = 4, 4 + 4 * NC
+
+    pl.semaphore_wait(barrier, 7 + 15 + NH - 1)
+    hop_z(stag_e, mid_e, 0)
+    loads[4].wait()
+    gather(0)
+
+    for i in (3, 0, 1, 2) + tuple(range(6, 19)):
+        loads[i].wait()
+    xf = x_ref[...].astype(F32)
+    xs[:, 8:24, :] = xf
+    xs[:, 0:8, :] = jnp.zeros((REQ, 8, WIDTH), F32)
+    prev = xs[:, 7:23, :]
+
+    def mix(cur, before, ratio):
+        return (cur + (before - cur) * ratio).astype(BF16)
+
+    delta_rows = (REQ * STEPS, WIDTH)
+    md = mix(xf, prev, ratio_d[...].reshape(1, 1, WIDTH)).reshape(delta_rows)
+    mr = mix(xf, prev, ratio_r[...].reshape(1, 1, WIDTH)).reshape(delta_rows)
+    pb[0] = mm(left_d[...], md, NT).astype(BF16)
+    pb[1] = mm(left_r[...], mr, NT).astype(BF16)
+    def to_heads(src, dst, n):
+        for i in range(1, NH):
+            pltpu.make_async_remote_copy(
+                src_ref=src(lax.rem(hd + i, NH)), dst_ref=dst.at[hd], send_sem=ss_h.at[n], recv_sem=rs_h.at[n],
+                device_id=(me, lax.rem(hd + i, NH)), device_id_type=MESH,
+            ).start()
+
+    def heads_of(dst, n):
+        return pltpu.make_async_remote_copy(
+            src_ref=dst.at[pl.ds(0, NH - 1)], dst_ref=dst.at[pl.ds(0, NH - 1)],
+            send_sem=ss_h.at[n], recv_sem=rs_h.at[n], device_id=(me, hd), device_id_type=MESH,
+        )
+
+    def part(g):
+        return rq_ref.at[:, :, pl.ds(pl.multiple_of(g * WIDTH, WIDTH), WIDTH)]
+
+    to_heads(lambda g: pb, pr, 1)
+    to_heads(part, r_recv, 0)
+    all_z(stag_e, mid_e, 0).wait_recv()
+    hop_w(mid_e, recv_e, 1)
+    for cc in range(1, NC):
+        gather(cc)
+
     row8 = lax.broadcasted_iota(I32, (REQ, 1024), 0)
     lane1024 = lax.broadcasted_iota(I32, (REQ, 1024), 1)
     q_of = jnp.zeros((REQ, 1024), I32)
@@ -177,71 +271,6 @@
     from_holder = hot(sub_f == holder)
     to_owner = hot(sub_f == owner)
 
-    loads[4].wait()
-    loads[5].wait()
-    edges = jnp.concatenate([ed_ref[...], jnp.zeros((96, 128), F32)], axis=0).astype(BF16)
-    stag_e[...] = mm(pick, edges, NT).reshape(8, 16, 1, 128)
-
-    def lay(dst, src, ct):
-        for c in range(ct):
-            tr_s[pl.ds(c, NB, stride=ct), :] = src[:, c * 128 : (c + 1) * 128]
-        dst[...] = tr_s[pl.ds(0, NB * ct), :].reshape(dst.shape).astype(BF16)
-
-    for cc in range(NC):
-        lay(stag.at[cc], mm(pick, st_ref[:, cc * CW : (cc + 1) * CW].astype(BF16)), CT)
-
-    def first_hop(src, dst, cc, n):
-        (hop_w if cc % 2 else hop_z)(src.at[cc], dst.at[cc], n + 2 * cc)
-
-    def first_all(src, dst, cc, n):
-        return (all_w if cc % 2 else all_z)(src.at[cc], dst.at[cc], n + 2 * cc)
-
-    def second_hop(src, dst, cc, n):
-        (hop_z if cc % 2 else hop_w)(src.at[cc], dst.at[cc], n + 1 + 2 * cc)
-
-    def second_all(src, dst, cc, n):
-        return (all_z if cc % 2 else all_w)(src.at[cc], dst.at[cc], n + 1 + 2 * cc)
-
-    fetch_n, back_n = 4, 4 + 2 * NC
-
-    for i in (3, 0, 1, 2) + tuple(range(6, 19)):
-        loads[i].wait()
-    xf = x_ref[...].astype(F32)
-    xs[:, 8:24, :] = xf
-    xs[:, 0:8, :] = jnp.zeros((REQ, 8, WIDTH), F32)
-    prev = xs[:, 7:23, :]
-
-    def mix(cur, before, ratio):
-        return (cur + (before - cur) * ratio).astype(BF16)
-
-    delta_rows = (REQ * STEPS, WIDTH)
-    md = mix(xf, prev, ratio_d[...].reshape(1, 1, WIDTH)).reshape(delta_rows)
-    mr = mix(xf, prev, ratio_r[...].reshape(1, 1, WIDTH)).reshape(delta_rows)
-    pb[0] = mm(left_d[...], md, NT).astype(BF16)
-    pb[1] = mm(left_r[...], mr, NT).astype(BF16)
-    def to_heads(src, dst, n):
-        for i in range(1, NH):
-            pltpu.make_async_remote_copy(
-                src_ref=src(lax.rem(hd + i, NH)), dst_ref=dst.at[hd], send_sem=ss_h.at[n], recv_sem=rs_h.at[n],
-                device_id=(me, lax.rem(hd + i, NH)), device_id_type=MESH,
-            ).start()
-
-    def heads_of(dst, n):
-        return pltpu.make_async_remote_copy(
-            src_ref=dst.at[pl.ds(0, NH - 1)], dst_ref=dst.at[pl.ds(0, NH - 1)],
-            send_sem=ss_h.at[n], recv_sem=rs_h.at[n], device_id=(me, hd), device_id_type=MESH,
-        )
-
-    def part(g):
-        return rq_ref.at[:, :, pl.ds(pl.multiple_of(g * WIDTH, WIDTH), WIDTH)]
-
-    pl.semaphore_wait(barrier, 7 + 15 + NH - 1)
-    hop_z(stag_e, mid_e, 0)
-    to_heads(part, r_recv, 0)
-    to_heads(lambda g: pb, pr, 1)
-    first_hop(stag, mid, 0, fetch_n)
-    first_hop(stag, mid, 1, fetch_n)
-
     pr[pl.ds(hd, 1)] = pb[...].reshape(1, 2, 96, 128)
     r_recv[pl.ds(hd, 1)] = rq_ref[:, :, pl.ds(pl.multiple_of(hd * WIDTH, WIDTH), WIDTH)].reshape(
         1, REQ, 4, WIDTH
@@ -315,18 +344,12 @@
 
     lax.fori_loop(0, 4, turn_values, 0)
 
-    all_z(stag_e, mid_e, 0).wait_recv()
-    hop_w(mid_e, recv_e, 1)
-    first_hop(stag, mid, 2, fetch_n)
-    first_hop(stag, mid, 3, fetch_n)
     lax.fori_loop(1, 8, turn_pair, 0)
 
     def pass_on(cc):
-        first_all(stag, mid, cc, fetch_n).wait_recv()
-        second_hop(mid, recv, cc, fetch_n)
+        second_hop(stag, mid, recv, cc, fetch_n)
 
     pass_on(0)
-    pass_on(1)
 
     all_w(mid_e, recv_e, 1).wait_recv()
     by_item = mm(from_holder, recv_e[...].reshape(NB, 128).astype(BF16), TN)
@@ -344,6 +367,7 @@
     pb0[0, :, 0:96] = mm(mix(x0, edge, ratio_d[...]), left_d[...], NT)
     pb0[1, :, 0:96] = mm(mix(x0, edge, ratio_r[...]), left_r[...], NT)
     to_heads(lambda g: pb0, pr0, 2)
+    pass_on(1)
     pr0[pl.ds(hd, 1)] = pb0[...].reshape(1, 2, REQ, 128)
 
 
@@ -361,8 +385,6 @@
     back_es[...] = mm(to_owner, items.astype(BF16)).reshape(8, 16, 1, 128)
     hop_z(back_es, back_em, 2)
 
-    pass_on(2)
-    pass_on(3)
     heads_of(pr0, 2).wait_recv()
     sums0 = (pr0[0] + pr0[1] + pr0[2] + pr0[3])[:, :, :96]
     keep0, rate0 = second(sums0[0], sums0[1], NN)
@@ -371,6 +393,7 @@
     put_step(a_r, 0, rate0)
     put_step(k_r, 0, k0 * (1.0 + (rate0 - 1.0) * written[...]))
     turn_pair(0, 0)
+    pass_on(2)
 
     def advance_rows(row0, local0):
         start = [st_t[pl.ds(pl.multiple_of((local0 + i) * HW, HW), HW), :] for i in range(RB)]
@@ -392,17 +415,17 @@
                 out.append(s)
             return tuple(out)
 
-        lax.fori_loop(0, STEPS, step, tuple(start))
+        lax.fori_loop(0, STEPS, step, tuple(start), unroll=4)
 
     def return_on(cc):
-        first_all(back_s, back_m, cc, back_n).wait_recv()
-        second_hop(back_m, back_r, cc, back_n)
+        second_hop(back_s, back_m, back_r, cc, back_n)
 
     for cc in range(NC):
-        second_all(mid, recv, cc, fetch_n).wait_recv()
-        tr_s[...] = recv[cc].astype(F32).reshape(NB * CT, 128)
+        received(second_all(mid, recv, cc, fetch_n))
+        for half in range(2):
+            tr_s[half * NB * CS : (half + 1) * NB * CS, :] = recv[cc, half].astype(F32).reshape(NB * CS, 128)
         for c in range(CT):
-            block = tr_s[pl.ds(c, NB, stride=CT), :].astype(BF16)
+            block = tr_s[pl.ds(c // CS * NB * CS + c % CS, NB, stride=CS), :].astype(BF16)
             st_t[c * 128 : (c + 1) * 128, :] = mm(block, from_holder, TN)
 
         def rows(ib, carry, cc=cc):
@@ -410,9 +433,10 @@
             return carry
 
         lax.fori_loop(0, CROWS // RB, rows, 0)
-        lay(back_s.at[cc], mm(to_owner, kept[...].astype(BF16), NT), CT)
+        lay_piece(back_s.at[cc], mm(to_owner, kept[...].astype(BF16), NT))
         first_hop(back_s, back_m, cc, back_n)
         if cc == 0:
+            pass_on(3)
             all_z(back_es, back_em, 2).wait_recv()
             hop_w(back_em, back_er, 3)
         if cc >= 2:
@@ -454,16 +478,16 @@
 
     all_w(back_em, back_er, 3).wait_recv()
     for cc in range(NC):
-        second_all(back_m, back_r, cc, back_n).wait_recv()
+        received(second_all(back_m, back_r, cc, back_n))
     all_z(stag_e, mid_e, 0).wait_send()
     all_w(mid_e, recv_e, 1).wait_send()
     all_z(back_es, back_em, 2).wait_send()
     all_w(back_em, back_er, 3).wait_send()
     for cc in range(NC):
-        first_all(stag, mid, cc, fetch_n).wait_send()
-        second_all(mid, recv, cc, fetch_n).wait_send()
-        first_all(back_s, back_m, cc, back_n).wait_send()
-        second_all(back_m, back_r, cc, back_n).wait_send()
+        sent(first_all(stag, mid, cc, fetch_n))
+        sent(second_all(mid, recv, cc, fetch_n))
+        sent(first_all(back_s, back_m, cc, back_n))
+        sent(second_all(back_m, back_r, cc, back_n))
     heads_of(r_recv, 0).wait_send()
     heads_of(pr, 1).wait_send()
     heads_of(pr0, 2).wait_send()
@@ -475,9 +499,10 @@
     ne_ref[...] = mm(back_er[...].reshape(NB, 128).astype(BF16), put, TN)[0:32]
     put_t = jnp.transpose(put.astype(F32)).astype(BF16)
     for cc in range(NC):
-        tr_s[...] = back_r[cc].astype(F32).reshape(NB * CT, 128)
+        for half in range(2):
+            tr_s[half * NB * CS : (half + 1) * NB * CS, :] = back_r[cc, half].astype(F32).reshape(NB * CS, 128)
         for c in range(CT):
-            block = tr_s[pl.ds(c, NB, stride=CT), :].astype(BF16)
+            block = tr_s[pl.ds(c // CS * NB * CS + c % CS, NB, stride=CS), :].astype(BF16)
             at = cc * CW + c * 128
             ns_ref[:, at : at + 128] = mm(put_t, block)
 
@@ -513,7 +538,7 @@
         kernel,
         out_shape=(
             jax.ShapeDtypeStruct((REQ, STEPS, WIDTH), BF16),
-            jax.ShapeDtypeStruct((NC, 8, 16, CT, 128), BF16),
+            jax.ShapeDtypeStruct((NC, 2, 8, 16, CS, 128), BF16),
             jax.ShapeDtypeStruct((8, 16, 1, 128), F32),
             jax.ShapeDtypeStruct((NB, 128), BF16),
         ),
@@ -523,14 +548,14 @@
         + [pltpu.SMEM(a.shape, a.dtype) for a in arrays[-2:]]
         + [
             dma((NI,)),
-            pltpu.VMEM((NC, 8, 16, CT, 128), BF16),
-            pltpu.VMEM((NC, 8, 16, CT, 128), BF16),
-            pltpu.VMEM((NC, 8, 16, CT, 128), BF16),
+            pltpu.VMEM((NC, 2, 8, 16, CS, 128), BF16),
+            pltpu.VMEM((NC, 2, 8, 16, CS, 128), BF16),
+            pltpu.VMEM((NC, 2, 8, 16, CS, 128), BF16),
             pltpu.VMEM((8, 16, 1, 128), F32),
             pltpu.VMEM((8, 16, 1, 128), F32),
             pltpu.VMEM((8, 16, 1, 128), F32),
-            pltpu.VMEM((NC, 8, 16, CT, 128), BF16),
-            pltpu.VMEM((NC, 8, 16, CT, 128), BF16),
+            pltpu.VMEM((NC, 2, 8, 16, CS, 128), BF16),
+            pltpu.VMEM((NC, 2, 8, 16, CS, 128), BF16),
             pltpu.VMEM((8, 16, 1, 128), F32),
             pltpu.VMEM((8, 16, 1, 128), F32),
             pltpu.VMEM((NH, REQ, 4, WIDTH), BF16),
@@ -559,7 +584,7 @@
             pltpu.VMEM((STEPS, HW, 128), F32),
             pltpu.VMEM((STEPS, ROWS, 128), F32),
             pltpu.VMEM((STEPS, ROWS, 128), F32),
-            dma((4 + 4 * NC,)), dma((4 + 4 * NC,)), dma((3,)), dma((3,)),
+            dma((4 + 8 * NC,)), dma((4 + 8 * NC,)), dma((3,)), dma((3,)),
         ],
         compiler_params=pltpu.CompilerParams(
             collective_id=0, has_side_effects=True, vmem_limit_bytes=24 << 20

time: 58.5 us -> 54 us (0.923)
  Pallas kernels: 57.7 us -> 53.3 us
    pallas_call x1, Pallas kernels: 56.3 us -> 51.6 us  [local(): pl.pallas_call(kernel, out_shape=(jax.ShapeDtypeStruct((REQ, STEPS, WIDTH...]
where the time goes in v3:
time: 54 us; the launch traced here: 53.9 us
  Pallas kernels  53.3 us (99%)
  between operations  0.65 us (1%)
    pallas_call x1, Pallas kernels, local(): pl.pallas_call(kernel, out_shape=(jax.ShapeDtypeStruct((REQ, STEPS, WIDTH...  51.6 us
    pallas_call x1, Pallas kernels, local(): pl.pallas_call(settle, out_shape=(jax.ShapeDtypeStruct((REQ, STEPS, WIDTH...  1.63 us

profile of v3, /device:TPU:1, one launch (start us, length us, event | category | flops | bytes accessed | tf_op | source)
XLA Modules:
  0.0 53.9 jit_solution(11758219495342712784)
XLA Ops:
  0.6 51.6 %draft_check.1 = (bf16[8,16,512]{2,1,0:T(8,128)(2,1)S(1)}, bf16[4,2,8,16,2,128]{5,4,3,2,1,0:T(2,128)(2,1)S(1)}, f32[8,16,1,128]{3,2,1,0:T(1,128)S(1)}, bf16[128,128]{1,0:T(8,128)(2,1)S(1)}) custom-call(bf16[8,16,512]{2,1,0:T(8,128)(2,1)} %refs_0_.1, bf16[8,16,512]{2,1,0:T(8,128)(2,1)} %refs_1_.1, bf16[8,16,512]{2,1,0:T(8,128)(2,1)} %refs_2_.1, ...), custom_call_target="tpu_custom_call" | custom-call | tf_op jit(solution)/shard_map/draft_check/pallas_call | solution.py:537
  52.3 1.6 %settle.1 = (bf16[8,16,512]{2,1,0:T(8,128)(2,1)}, f32[128,2048]{1,0:T(8,128)}, f32[32,128]{1,0:T(8,128)}) custom-call(bf16[8,16,512]{2,1,0:T(8,128)(2,1)S(1)} %get-tuple-element.10.tb_ref, bf16[4,2,8,16,2,128]{5,4,3,2,1,0:T(2,128)(2,1)S(1)} %get-tuple-element.11.back_r, f32[8,16,1,128]{3,2,1,0:T(1,128)S(1)} %get-tuple-element.12.back_er, ...), custom_call_target="tpu_custom_call" | custom-call | tf_op jit(solution)/shard_map/settle/pallas_call | solution.py:596
